TPU v7x, 512 devices: a whole 4x8x8 slice. The times are simulated.
512 devices in a mesh: gx: 8 (over z), gy: 8 (over x, core), gz: 8 (over y).
Axes of the slice: x: 4, y: 8, z: 8, core: 2. Of those that a mesh axis runs over, the one named last changes fastest.
Arguments:
- features: bfloat16 [8, 8, 8, 512, 128], P('gx', 'gy', 'gz'), may hold values from -6 to 6
- coords: float32 [8, 8, 8, 3, 512], P('gx', 'gy', 'gz'), as said below
- counts: int32 [8, 8, 8], P('gx', 'gy', 'gz'), may hold values from 128 to 512, as said below
- sources: int32 [8, 8, 8, 512], P('gx', 'gy', 'gz'), may hold values from 0 to 13823, as said below
- wanted: int32 [8, 8, 8, 2, 27, 1], P('gx', 'gy', 'gz'), may hold values from 0 to 7, as said below
- pairs: int32 [8, 8, 8, 2, 32], P('gx', 'gy', 'gz'), may hold values from 0 to 34, as said below
- lifting_weight: bfloat16 [2, 128, 128], replicated, may hold values from -0.5 to 0.5
- radial_weight: float32 [2, 3, 8, 128], replicated, may hold values from -2 to 2
- mix_weight: float32 [2, 3, 128], replicated, may hold values from -3 to 3
- out_weight: bfloat16 [2, 128, 128], replicated, may hold values from -0.5 to 0.5
- force_weight: float32 [8], replicated, may hold values from -4 to 4
Outputs:
- updated: bfloat16 [8, 8, 8, 512, 128], P('gx', 'gy', 'gz')
- forces: float32 [8, 8, 8, 3, 512], P('gx', 'gy', 'gz')
Inputs may be any that keep to these rules, and one draw needn't show every extreme that they name: `counts`: some device holds exactly 512 live atoms. `sources`: the neighbour code of a value is value // 512 and its slot value % 512; every record of every device is taken by exactly one new slot. `wanted`: the 1 tiles read from one neighbour code in one layer are distinct. `pairs`: row 0 is below 8; a row 1 value v below 8 is an own tile, otherwise ghost slot (v - 8) % 1 of code (v - 8), never code 13. `coords`: each component lies in the cell, from 0 to 5120 ** (1/3), except for records taken by another device, which lie up to 1 outside the face toward their new owner.
All inputs are finite; a program needn't handle non-finite values.
Results may differ from a plain program's by a relative error of at most 0.0061.
Values may be sent and summed in bfloat16 or wider, within the bound.
A program may use at most 64 MiB of HBM per device.

v0:
```python
import math

import jax
import jax.numpy as jnp
import numpy as np
from jax import lax
from jax.sharding import PartitionSpec as P

NB = 8
TILE = 64
LAYERS = 2
PAIR_BLOCK = 2


CUTOFF = 5.0
BASIS_WIDTH = 0.6
MESSAGE_SCALE = 0.2
SOFTENING = 0.25
FAR_AWAY = 1000.0
DEAD_SPACING = 100.0
DENSITY = 0.1


def padded(cells, sides, width):
    for axis, dim in sides:
        count = lax.axis_size(axis)
        head = lax.slice_in_dim(cells, 0, width, axis=dim)
        tail = lax.slice_in_dim(cells, cells.shape[dim] - width, cells.shape[dim], axis=dim)
        cells = jnp.concatenate(
            [
                lax.ppermute(tail, axis, [(i, (i + 1) % count) for i in range(count)]),
                cells,
                lax.ppermute(head, axis, [((i + 1) % count, i) for i in range(count)]),
            ],
            axis=dim,
        )
    return cells


def offset_table():
    return np.array(
        [
            [first_step, second_step, third_step]
            for first_step in (-1, 0, 1)
            for second_step in (-1, 0, 1)
            for third_step in (-1, 0, 1)
        ],
        dtype=np.float32,
    )


def harmonics(direction):
    along_x = direction[0]
    along_y = direction[1]
    along_z = direction[2]
    root_three = math.sqrt(3.0)
    root_five = math.sqrt(5.0)
    root_fifteen = math.sqrt(15.0)
    return jnp.stack(
        [
            jnp.ones_like(along_x),
            root_three * along_x,
            root_three * along_y,
            root_three * along_z,
            root_fifteen * along_x * along_y,
            root_fifteen * along_y * along_z,
            0.5 * root_five * (3.0 * along_z * along_z - 1.0),
            root_fifteen * along_x * along_z,
            0.5 * root_fifteen * (along_x * along_x - along_y * along_y),
        ]
    )


def multiply(left, right):
    return jnp.dot(left, right, preferred_element_type=jnp.float32)


def pair_terms(place_i, place_j, rows_i, rows_j, same_tile, radial_layer, force_weight, with_force):
    tile_size = place_i.shape[1]
    channels = rows_j.shape[1]
    wide_count = NB * tile_size
    place_wide = jnp.tile(place_j, (1, NB))
    separation = place_i[:, :, None] - place_wide[:, None, :]
    distance = jnp.sqrt(jnp.sum(separation * separation, axis=0) + SOFTENING)
    direction = separation / distance[None]
    centers = jnp.repeat(0.5 + jnp.arange(NB).astype(jnp.float32) * (4.2 / (NB - 1)), tile_size)
    ratio = jnp.minimum(distance / CUTOFF, 1.0)
    envelope = (1.0 - ratio * ratio) ** 2
    scaled = (distance - centers[None, :]) / BASIS_WIDTH
    keep_mask = 1.0 - same_tile * jnp.tile(jnp.eye(tile_size, dtype=jnp.float32), (1, NB))
    basis = jnp.exp(-scaled * scaled) * envelope * keep_mask
    angular = harmonics(direction)
    edges = (angular * basis[None]).astype(jnp.bfloat16)
    weighted = (radial_layer[:, :, None, :] * rows_j.astype(jnp.float32)[None, None]).astype(
        jnp.bfloat16
    )
    weighted = weighted.reshape(3, wide_count, channels)
    groups = ((0, 1), (1, 4), (4, 9))
    pieces = []
    for degree in range(3):
        start_row, stop_row = groups[degree]
        edge_block = edges[start_row:stop_row].reshape(
            (stop_row - start_row) * tile_size, wide_count
        )
        pieces.append(
            multiply(edge_block, weighted[degree]).reshape(
                stop_row - start_row, tile_size, channels
            )
        )
    message = jnp.concatenate(pieces, axis=0) * MESSAGE_SCALE
    if with_force:
        intersection = multiply(rows_i, rows_j.T) / math.sqrt(channels)
        basis_split = jnp.transpose(basis.reshape(tile_size, NB, tile_size), (1, 0, 2))
        profile = jnp.sum(force_weight[:, None, None] * basis_split, axis=0)
        narrow_direction = direction[:, :, :tile_size]
        pushes = (profile * intersection)[None] * narrow_direction
        return (message, 0.5 * jnp.sum(pushes, axis=2), -0.5 * jnp.sum(pushes, axis=1))
    nothing = jnp.zeros((3, tile_size), jnp.float32)
    return (message, nothing, nothing)


def update(hidden_features, totals, mix_layer, out_layer):
    channels = hidden_features.shape[1]
    scalar_part = totals[:, 0]
    vector_part = jnp.sum(totals[:, 1:4] ** 2, axis=1)
    tensor_part = jnp.sum(totals[:, 4:9] ** 2, axis=1)
    mixed = mix_layer[0] * scalar_part + mix_layer[1] * vector_part + mix_layer[2] * tensor_part
    active = jax.nn.silu(mixed).astype(jnp.bfloat16).reshape(-1, channels)
    return (hidden_features.astype(jnp.float32) + multiply(active, out_layer)).astype(jnp.bfloat16)


def opposite(grown, shape_out):
    return grown[0::2, 0::2, 0::2].reshape(shape_out)


def beside_all(placed):
    grown = padded(placed, (("gx", 0), ("gy", 1), ("gz", 2)), 1)
    return grown.reshape(27, 3, placed.shape[4])


def relay_rows(bundle):
    bundle = padded(bundle, (("gx", 0),), 1)[0::2]
    bundle = padded(bundle, (("gy", 1),), 1)[:, 0::2]
    return padded(bundle, (("gz", 2),), 1)[:, :, 0::2]


def relayed_force(bundle):
    bundle = padded(bundle, (("gx", 0),), 1)[0::2]
    bundle = padded(bundle, (("gy", 1),), 1)[:, 0::2]
    return padded(bundle, (("gz", 2),), 1)[:, :, 0::2]


def body(
    features,
    coords,
    counts,
    sources,
    wanted,
    pairs,
    lifting_weight,
    radial_weight,
    mix_weight,
    out_weight,
    force_weight,
):
    slot_count = features.shape[3]
    channels = features.shape[4]
    tile_count = slot_count // TILE
    ghost_count = wanted.shape[5]
    pair_count = pairs.shape[4]
    cell_edge = (slot_count / DENSITY) ** (1.0 / 3.0)
    shifts = jnp.asarray(offset_table()) * cell_edge
    slot_index = jnp.arange(slot_count)
    dead_place = FAR_AWAY + DEAD_SPACING * slot_index.astype(jnp.float32)
    start_place = jnp.where(
        slot_index[None, :] < counts.reshape(()), coords.reshape(3, slot_count), dead_place[None, :]
    )
    anchor = sources.reshape(slot_count)
    gathered_rows = padded(features, (("gx", 0), ("gy", 1), ("gz", 2)), 1)
    hidden_features = jnp.take(gathered_rows.reshape(27 * slot_count, channels), anchor, axis=0)
    nearby_start = beside_all(start_place.reshape(1, 1, 1, 3, slot_count)) + shifts[:, :, None]
    places = jnp.take(
        jnp.transpose(nearby_start, (1, 0, 2)).reshape(3, 27 * slot_count), anchor, axis=1
    )
    nearby = beside_all(places.reshape(1, 1, 1, 3, slot_count)) + shifts[:, :, None]
    nearby_tiles = jnp.transpose(nearby.reshape(27, 3, tile_count, TILE), (0, 2, 1, 3)).reshape(
        27 * tile_count, 3, TILE
    )
    local_places = jnp.transpose(places.reshape(3, tile_count, TILE), (1, 0, 2))
    lists = wanted.reshape(LAYERS, 27, ghost_count)
    pair_list = pairs.reshape(2, pair_count)
    code_base = (jnp.arange(27) * tile_count)[:, None]
    cube_lists = jnp.transpose(lists, (1, 0, 2)).reshape(3, 3, 3, LAYERS, ghost_count)
    grown_lists = padded(cube_lists, (("gx", 0), ("gy", 1), ("gz", 2)), 1)
    requests = opposite(grown_lists, (27, LAYERS, ghost_count))
    partial_force = jnp.zeros((tile_count + 27 * ghost_count, 3, TILE), jnp.float32)
    for index_of_layer in range(LAYERS):
        projected_features = multiply(hidden_features, lifting_weight[index_of_layer]).astype(
            jnp.bfloat16
        )
        projected_tiles = projected_features.reshape(tile_count, TILE, channels)
        picked = (code_base + lists[index_of_layer]).reshape(-1)
        outgoing = jnp.take(projected_tiles, requests[:, index_of_layer].reshape(-1), axis=0)
        relayed = relay_rows(outgoing.reshape(3, 3, 3, ghost_count, TILE, channels))
        ghost_rows = relayed.reshape(27 * ghost_count, TILE, channels)
        ghost_places = jnp.take(nearby_tiles, picked, axis=0)
        source_rows = jnp.concatenate([projected_tiles, ghost_rows], axis=0)
        source_places = jnp.concatenate([local_places, ghost_places], axis=0)
        with_force = index_of_layer == LAYERS - 1
        radial_layer = radial_weight[index_of_layer]

        def pair_values(place_i, place_j, rows_i, rows_j, same_tile):
            return pair_terms(
                place_i, place_j, rows_i, rows_j, same_tile, radial_layer, force_weight, with_force
            )

        batched = jax.vmap(pair_values)

        def one_block(block_index, carried):
            totals, partial_value = carried
            targets = lax.dynamic_slice_in_dim(pair_list[0], block_index * PAIR_BLOCK, PAIR_BLOCK)
            anchors = lax.dynamic_slice_in_dim(pair_list[1], block_index * PAIR_BLOCK, PAIR_BLOCK)
            same_tile = (targets == anchors).astype(jnp.float32)
            message, on_target, on_source = batched(
                source_places[targets],
                source_places[anchors],
                source_rows[targets],
                source_rows[anchors],
                same_tile,
            )
            totals = totals.at[targets].add(message)
            partial_value = partial_value.at[targets].add(on_target).at[anchors].add(on_source)
            return (totals, partial_value)

        initial = (
            jnp.zeros((tile_count, 9, TILE, channels), jnp.float32),
            jnp.zeros((tile_count + 27 * ghost_count, 3, TILE), jnp.float32),
        )
        totals, partial_force = lax.fori_loop(0, pair_count // PAIR_BLOCK, one_block, initial)
        hidden_features = update(
            hidden_features, totals, mix_weight[index_of_layer], out_weight[index_of_layer]
        )
    own_force = partial_force[:tile_count]
    ghost_force = partial_force[tile_count:].reshape(27, ghost_count, 3 * TILE)
    tile_ids = jnp.arange(tile_count)
    arrived = relayed_force(ghost_force.reshape(3, 3, 3, ghost_count, 3 * TILE)).reshape(
        27, ghost_count, 3 * TILE
    )
    marks = (requests[:, LAYERS - 1][:, :, None] == tile_ids[None, None, :]).astype(jnp.float32)
    returned = jnp.einsum("cgt,cgx->tx", marks, arrived, precision=lax.Precision.HIGHEST)
    total_force = own_force + returned.reshape(tile_count, 3, TILE)
    forces = jnp.transpose(total_force, (1, 0, 2)).reshape(1, 1, 1, 3, slot_count)
    return (hidden_features.reshape(1, 1, 1, slot_count, channels), forces)


def solution(mesh):
    placed = (
        P("gx", "gy", "gz", None, None),
        P("gx", "gy", "gz", None, None),
        P("gx", "gy", "gz"),
        P("gx", "gy", "gz", None),
        P("gx", "gy", "gz", None, None, None),
        P("gx", "gy", "gz", None, None),
        P(),
        P(),
        P(),
        P(),
        P(),
    )
    return jax.shard_map(
        body,
        mesh=mesh,
        in_specs=placed,
        out_specs=(P("gx", "gy", "gz", None, None), P("gx", "gy", "gz", None, None)),
        check_vma=False,
    )
```

profile of v0, /device:TPU:1, one launch (start us, length us, event | category | flops | bytes accessed | tf_op | source)
XLA Modules:
  0.0 578.2 jit_solution(10692208238571222071)
XLA Ops:
  0.6 4.8 collective-permute-start
  5.5 8.6 %collective-permute-start.1 = (bf16[1,1,1,512,128]{4,3,2,1,0:T(8,128)(2,1)}, bf16[1,1,1,512,128]{4,3,2,1,0:T(8,128)(2,1)S(1)}, u32[]{:S(2)}, u32[]{:S(2)}) collective-permute-start(bf16[1,1,1,512,128]{4,3,2,1,0:T(8,128)(2,1)} %param.20), channel_id=1, source_target_pairs={{64,0},{128,64},{192,128},{256,192},{320,256},{384,320},{448,384},... | collective-permute-start | bytes 393224 | tf_op jit(solution)/shard_map/ppermute | solution.py:33
  17.0 4.6 collective-permute-start.19
  40.0 3.2 collective-permute-start.22
  43.3 3.8 collective-permute-start.23
  47.1 4.9 collective-permute-start.7
  60.1 4.6 collective-permute-start.11
  67.1 2.9 collective-permute-start.4
  70.0 4.1 collective-permute-start.5
  75.5 5.1 copy.146
  80.6 4.0 gather_fusion.8
  87.4 5.1 collective-permute-start.13
  95.9 3.4 collective-permute-start.14
  102.8 2.8 collective-permute-start.16
  105.7 3.7 collective-permute-start.17
  120.6 3.7 collective-permute-start.24
  124.3 3.5 collective-permute-start.25
  130.7 2.8 collective-permute-start.26
  138.2 3.7 collective-permute-start.28
  142.0 2.8 collective-permute-start.29
  149.8 131.3 %while.32 = (s32[]{:T(128)}, f32[8,9,64,128]{3,2,1,0:T(8,128)}, s32[2,32]{1,0:T(2,128)}, f32[35,3,64]{2,1,0:T(4,128)S(1)}, f32[1,3,8,128]{3,2,1,0:T(8,128)S(1)},...) while((s32[]{:T(128)}, f32[8,9,64,128]{3,2,1,0:T(8,128)}, ...), condition=%wide.region_3.6_spmd, body=%wide.region_0.5_spmd.sunk | while | flops 156510256 | bytes 25273684 | solution.py:239
  286.8 3.2 collective-permute-start.30
  290.0 3.6 collective-permute-start.31
  296.1 4.4 collective-permute-start.32
  305.2 4.2 collective-permute-start.34
  312.4 3.4 collective-permute-done.35
  318.3 234.6 %while.33 = (s32[]{:T(128)}, f32[8,9,64,128]{3,2,1,0:T(8,128)}, f32[35,3,64]{2,1,0:T(4,128)}, s32[2,32]{1,0:T(2,128)}, f32[35,3,64]{2,1,0:T(4,128)S(1)}, /*index...) while((s32[]{:T(128)}, f32[8,9,64,128]{3,2,1,0:T(8,128)}, ...), condition=%wide.region_14.17_spmd, body=%wide.region_6.16_spmd.sunk | while | flops 159673136 | bytes 26677500 | solution.py:239
  553.9 3.4 collective-permute-start.36
  557.3 3.6 collective-permute-start.37
  565.3 3.3 collective-permute-start.39
  569.7 2.9 collective-permute-start.40
  572.7 3.6 collective-permute-start.41
  (2103 shorter events, 449.4 us)
Async XLA Ops:
  0.6 53.6 %collective-permute-start = (bf16[1,1,1,512,128]{4,3,2,1,0:T(8,128)(2,1)}, bf16[1,1,1,512,128]{4,3,2,1,0:T(8,128)(2,1)S(1)}, u32[]{:S(2)}, u32[]{:S(2)}) collective-permute-start(bf16[1,1,1,512,128]{4,3,2,1,0:T(8,128)(2,1)} %param.20), channel_id=1, source_target_pairs={{0,64},{64,128},{128,192},{192,256},{256,320},{320,384},{384,448},... | collective-permute-start | bytes 393224 | tf_op jit(solution)/shard_map/ppermute | solution.py:31
  5.5 49.7 %collective-permute-start.1 = (bf16[1,1,1,512,128]{4,3,2,1,0:T(8,128)(2,1)}, bf16[1,1,1,512,128]{4,3,2,1,0:T(8,128)(2,1)S(1)}, u32[]{:S(2)}, u32[]{:S(2)}) collective-permute-start(bf16[1,1,1,512,128]{4,3,2,1,0:T(8,128)(2,1)} %param.20), channel_id=1, source_target_pairs={{64,0},{128,64},{192,128},{256,192},{320,256},{384,320},{448,384},... | collective-permute-start | bytes 393224 | tf_op jit(solution)/shard_map/ppermute | solution.py:33
  15.0 19.0 %collective-permute-start.18 = (s32[1,3,3,2,1]{2,1,3,4,0:T(4,128)S(1)}, s32[1,3,3,2,1]{2,1,3,4,0:T(4,128)S(1)}, u32[]{:S(2)}, u32[]{:S(2)}) collective-permute-start(s32[1,3,3,2,1]{2,1,3,4,0:T(4,128)S(1)} %slice.452), channel_id=1, source_target_pairs={{0,64},{64,128},{128,192},{192,256},{256,320},{320,384},{384,448},... | collective-permute-start | bytes 224 | tf_op jit(solution)/shard_map/ppermute | solution.py:31
  17.0 17.0 %collective-permute-start.19 = (s32[1,3,3,2,1]{2,1,0,3,4:T(4,128)S(1)}, s32[1,3,3,2,1]{2,1,0,3,4:T(4,128)S(1)}, u32[]{:S(2)}, u32[]{:S(2)}) collective-permute-start(s32[1,3,3,2,1]{2,1,0,3,4:T(4,128)S(1)} %bitcast.347), channel_id=1, source_target_pairs={{64,0},{128,64},{192,128},{256,192},{320,256},{384,320},{448,384},... | collective-permute-start | bytes 224 | tf_op jit(solution)/shard_map/ppermute | solution.py:33
  22.9 30.2 %collective-permute-start.6 = (f32[1,1,1,3,512]{4,2,3,1,0:T(1,128)S(1)}, f32[1,1,1,3,512]{4,2,3,1,0:T(1,128)S(1)}, u32[]{:S(2)}, u32[]{:S(2)}) collective-permute-start(f32[1,1,1,3,512]{4,2,3,1,0:T(1,128)S(1)} %broadcast_select_fusion.6), channel_id=1, source_target_pairs={{0,64},{64,128},{128,192},{192,256},{256,320},{320,384},{384,448},... | collective-permute-start | bytes 18440 | tf_op jit(solution)/shard_map/ppermute | solution.py:31
  40.0 7.0 %collective-permute-start.22 = (s32[5,5,1,2,1]{1,3,4,2,0:T(2,128)S(1)}, s32[5,5,1,2,1]{1,3,4,2,0:T(2,128)S(1)}, u32[]{:S(2)}, u32[]{:S(2)}) collective-permute-start(s32[5,5,1,2,1]{1,3,4,2,0:T(2,128)S(1)} %get-tuple-element.436), channel_id=1, source_target_pairs={{0,1},{1,2},{2,3},{3,4},{4,5},{5,6},{6,7},{7,0},{8,9},{9,10},{10,1... | collective-permute-start | bytes 608 | tf_op jit(solution)/shard_map/ppermute | solution.py:31
  43.3 8.7 %collective-permute-start.23 = (s32[5,5,1,2,1]{1,3,4,2,0:T(2,128)S(1)}, s32[5,5,1,2,1]{1,3,4,2,0:T(2,128)S(1)}, u32[]{:S(2)}, u32[]{:S(2)}) collective-permute-start(s32[5,5,1,2,1]{1,3,4,2,0:T(2,128)S(1)} %get-tuple-element.437), channel_id=1, source_target_pairs={{1,0},{2,1},{3,2},{4,3},{5,4},{6,5},{7,6},{0,7},{9,8},{10,9},{11,1... | collective-permute-start | bytes 608 | tf_op jit(solution)/shard_map/ppermute | solution.py:33
  47.1 6.0 %collective-permute-start.7 = (f32[1,1,1,3,512]{4,2,3,1,0:T(1,128)S(1)}, f32[1,1,1,3,512]{4,2,3,1,0:T(1,128)S(1)}, u32[]{:S(2)}, u32[]{:S(2)}) collective-permute-start(f32[1,1,1,3,512]{4,2,3,1,0:T(1,128)S(1)} %broadcast_select_fusion.6), channel_id=1, source_target_pairs={{64,0},{128,64},{192,128},{256,192},{320,256},{384,320},{448,384},... | collective-permute-start | bytes 18440 | tf_op jit(solution)/shard_map/ppermute | solution.py:33
  55.2 11.7 %collective-permute-start.2 = (bf16[3,1,1,512,128]{4,3,2,1,0:T(8,128)(2,1)S(1)}, bf16[3,1,1,512,128]{4,3,2,1,0:T(8,128)(2,1)S(1)}, u32[]{:S(2)}, u32[]{:S(2)}) collective-permute-start(bf16[3,1,1,512,128]{4,3,2,1,0:T(8,128)(2,1)S(1)} %constant_dynamic-update-slice_fusion), channel_id=1, source_target_pairs={{0,8},{8,16},{16,24},{24,32},{32,40},{40,48},{48,56},{56,0},{1,9},... | collective-permute-start | bytes 1179656 | tf_op jit(solution)/shard_map/ppermute | solution.py:31
  56.8 10.1 %collective-permute-start.3 = (bf16[3,1,1,512,128]{4,3,2,1,0:T(8,128)(2,1)S(1)}, bf16[3,1,1,512,128]{4,3,2,1,0:T(8,128)(2,1)S(1)}, u32[]{:S(2)}, u32[]{:S(2)}) collective-permute-start(bf16[3,1,1,512,128]{4,3,2,1,0:T(8,128)(2,1)S(1)} %constant_dynamic-update-slice_fusion), channel_id=1, source_target_pairs={{8,0},{16,8},{24,16},{32,24},{40,32},{48,40},{56,48},{0,56},{9,1},... | collective-permute-start | bytes 1179656 | tf_op jit(solution)/shard_map/ppermute | solution.py:33
  58.2 7.1 %collective-permute-start.10 = (f32[3,3,1,3,512]{4,2,3,1,0:T(1,128)S(1)}, f32[3,3,1,3,512]{4,2,3,1,0:T(1,128)S(1)}, u32[]{:S(2)}, u32[]{:S(2)}) collective-permute-start(f32[3,3,1,3,512]{4,2,3,1,0:T(1,128)S(1)} %pad_maximum_fusion.17), channel_id=1, source_target_pairs={{0,1},{1,2},{2,3},{3,4},{4,5},{5,6},{6,7},{7,0},{8,9},{9,10},{10,1... | collective-permute-start | bytes 165896 | tf_op jit(solution)/shard_map/ppermute | solution.py:31
  67.1 45.6 %collective-permute-start.4 = (bf16[3,3,1,512,128]{4,3,2,1,0:T(8,128)(2,1)S(1)}, bf16[3,3,1,512,128]{4,3,2,1,0:T(8,128)(2,1)S(1)}, u32[]{:S(2)}, u32[]{:S(2)}) collective-permute-start(bf16[3,3,1,512,128]{4,3,2,1,0:T(8,128)(2,1)S(1)} %pad_maximum_fusion.1), channel_id=1, source_target_pairs={{0,1},{1,2},{2,3},{3,4},{4,5},{5,6},{6,7},{7,0},{8,9},{9,10},{10,1... | collective-permute-start | bytes 3538952 | tf_op jit(solution)/shard_map/ppermute | solution.py:31
  70.0 43.8 %collective-permute-start.5 = (bf16[3,3,1,512,128]{4,3,2,1,0:T(8,128)(2,1)S(1)}, bf16[3,3,1,512,128]{4,3,2,1,0:T(8,128)(2,1)}, u32[]{:S(2)}, u32[]{:S(2)}) collective-permute-start(bf16[3,3,1,512,128]{4,3,2,1,0:T(8,128)(2,1)S(1)} %pad_maximum_fusion.1), channel_id=1, source_target_pairs={{1,0},{2,1},{3,2},{4,3},{5,4},{6,5},{7,6},{0,7},{9,8},{10,9},{11,1... | collective-permute-start | bytes 3538952 | tf_op jit(solution)/shard_map/ppermute | solution.py:33
  85.4 9.2 %collective-permute-start.12 = (f32[1,1,1,3,512]{3,4,2,1,0:T(8,128)S(1)}, f32[1,1,1,3,512]{3,4,2,1,0:T(8,128)S(1)}, u32[]{:S(2)}, u32[]{:S(2)}) collective-permute-start(f32[1,1,1,3,512]{3,4,2,1,0:T(8,128)S(1)} %bitcast_select_fusion), channel_id=1, source_target_pairs={{0,64},{64,128},{128,192},{192,256},{256,320},{320,384},{384,448},... | collective-permute-start | bytes 18440 | tf_op jit(solution)/shard_map/ppermute | solution.py:31
  87.4 8.4 %collective-permute-start.13 = (f32[1,1,1,3,512]{3,4,2,1,0:T(8,128)S(1)}, f32[1,1,1,3,512]{3,4,2,1,0:T(8,128)S(1)}, u32[]{:S(2)}, u32[]{:S(2)}) collective-permute-start(f32[1,1,1,3,512]{3,4,2,1,0:T(8,128)S(1)} %bitcast_select_fusion), channel_id=1, source_target_pairs={{64,0},{128,64},{192,128},{256,192},{320,256},{384,320},{448,384},... | collective-permute-start | bytes 18440 | tf_op jit(solution)/shard_map/ppermute | solution.py:33
  95.9 6.8 %collective-permute-start.14 = (f32[3,1,1,3,512]{4,2,3,1,0:T(1,128)S(1)}, f32[3,1,1,3,512]{4,2,3,1,0:T(1,128)S(1)}, u32[]{:S(2)}, u32[]{:S(2)}) collective-permute-start(f32[3,1,1,3,512]{4,2,3,1,0:T(1,128)S(1)} %pad_maximum_fusion.20), channel_id=1, source_target_pairs={{0,8},{8,16},{16,24},{24,32},{32,40},{40,48},{48,56},{56,0},{1,9},... | collective-permute-start | bytes 55304 | tf_op jit(solution)/shard_map/ppermute | solution.py:31
  102.8 7.8 %collective-permute-start.16 = (f32[3,3,1,3,512]{4,2,3,1,0:T(1,128)S(1)}, f32[3,3,1,3,512]{4,2,3,1,0:T(1,128)S(1)}, u32[]{:S(2)}, u32[]{:S(2)}) collective-permute-start(f32[3,3,1,3,512]{4,2,3,1,0:T(1,128)S(1)} %pad_maximum_fusion.18), channel_id=1, source_target_pairs={{0,1},{1,2},{2,3},{3,4},{4,5},{5,6},{6,7},{7,0},{8,9},{9,10},{10,1... | collective-permute-start | bytes 165896 | tf_op jit(solution)/shard_map/ppermute | solution.py:31
  105.7 6.0 %collective-permute-start.17 = (f32[3,3,1,3,512]{4,2,3,1,0:T(1,128)S(1)}, f32[3,3,1,3,512]{4,2,3,1,0:T(1,128)S(1)}, u32[]{:S(2)}, u32[]{:S(2)}) collective-permute-start(f32[3,3,1,3,512]{4,2,3,1,0:T(1,128)S(1)} %pad_maximum_fusion.18), channel_id=1, source_target_pairs={{1,0},{2,1},{3,2},{4,3},{5,4},{6,5},{7,6},{0,7},{9,8},{10,9},{11,1... | collective-permute-start | bytes 165896 | tf_op jit(solution)/shard_map/ppermute | solution.py:33
  120.6 8.9 %collective-permute-start.24 = (bf16[1,3,3,1,64,128]{5,4,2,1,0,3:T(8,128)(2,1)S(1)}, bf16[1,3,3,1,64,128]{5,4,2,1,0,3:T(8,128)(2,1)S(1)}, u32[]{:S(2)}, u32[]{:S(2)}) collective-permute-start(bf16[1,3,3,1,64,128]{5,4,2,1,0,3:T(8,128)(2,1)S(1)} %bitcast.336), channel_id=1, source_target_pairs={{0,64},{64,128},{128,192},{192,256},{256,320},{320,384},{384,448},... | collective-permute-start | bytes 442376 | tf_op jit(solution)/shard_map/ppermute | solution.py:31
  124.3 6.2 %collective-permute-start.25 = (bf16[1,3,3,1,64,128]{5,4,2,1,0,3:T(8,128)(2,1)S(1)}, bf16[1,3,3,1,64,128]{5,4,2,1,0,3:T(8,128)(2,1)S(1)}, u32[]{:S(2)}, u32[]{:S(2)}) collective-permute-start(bf16[1,3,3,1,64,128]{5,4,2,1,0,3:T(8,128)(2,1)S(1)} %bitcast.335), channel_id=1, source_target_pairs={{64,0},{128,64},{192,128},{256,192},{320,256},{384,320},{448,384},... | collective-permute-start | bytes 442376 | tf_op jit(solution)/shard_map/ppermute | solution.py:33
  130.7 6.2 %collective-permute-start.26 = (bf16[3,1,3,1,64,128]{5,4,2,1,0,3:T(8,128)(2,1)S(1)}, bf16[3,1,3,1,64,128]{5,4,2,1,0,3:T(8,128)(2,1)S(1)}, u32[]{:S(2)}, u32[]{:S(2)}) collective-permute-start(bf16[3,1,3,1,64,128]{5,4,2,1,0,3:T(8,128)(2,1)S(1)} %get-tuple-element.430), channel_id=1, source_target_pairs={{0,8},{8,16},{16,24},{24,32},{32,40},{40,48},{48,56},{56,0},{1,9},... | collective-permute-start | bytes 442376 | tf_op jit(solution)/shard_map/ppermute | solution.py:31
  138.2 7.1 %collective-permute-start.28 = (bf16[3,3,1,1,64,128]{5,4,2,1,0,3:T(8,128)(2,1)S(1)}, bf16[3,3,1,1,64,128]{5,4,2,1,0,3:T(8,128)(2,1)S(1)}, u32[]{:S(2)}, u32[]{:S(2)}) collective-permute-start(bf16[3,3,1,1,64,128]{5,4,2,1,0,3:T(8,128)(2,1)S(1)} %get-tuple-element.428), channel_id=1, source_target_pairs={{0,1},{1,2},{2,3},{3,4},{4,5},{5,6},{6,7},{7,0},{8,9},{9,10},{10,1... | collective-permute-start | bytes 442376 | tf_op jit(solution)/shard_map/ppermute | solution.py:31
  142.0 5.9 %collective-permute-start.29 = (bf16[3,3,1,1,64,128]{5,4,2,1,0,3:T(8,128)(2,1)S(1)}, bf16[3,3,1,1,64,128]{5,4,2,1,0,3:T(8,128)(2,1)S(1)}, u32[]{:S(2)}, u32[]{:S(2)}) collective-permute-start(bf16[3,3,1,1,64,128]{5,4,2,1,0,3:T(8,128)(2,1)S(1)} %get-tuple-element.429), channel_id=1, source_target_pairs={{1,0},{2,1},{3,2},{4,3},{5,4},{6,5},{7,6},{0,7},{9,8},{10,9},{11,1... | collective-permute-start | bytes 442376 | tf_op jit(solution)/shard_map/ppermute | solution.py:33
  286.8 7.4 %collective-permute-start.30 = (bf16[1,3,3,1,64,128]{5,4,2,1,0,3:T(8,128)(2,1)S(1)}, bf16[1,3,3,1,64,128]{5,4,2,1,0,3:T(8,128)(2,1)S(1)}, u32[]{:S(2)}, u32[]{:S(2)}) collective-permute-start(bf16[1,3,3,1,64,128]{5,4,2,1,0,3:T(8,128)(2,1)S(1)} %bitcast.338), channel_id=1, source_target_pairs={{0,64},{64,128},{128,192},{192,256},{256,320},{320,384},{384,448},... | collective-permute-start | bytes 442376 | tf_op jit(solution)/shard_map/ppermute | solution.py:31
  290.0 5.9 %collective-permute-start.31 = (bf16[1,3,3,1,64,128]{5,4,2,1,0,3:T(8,128)(2,1)S(1)}, bf16[1,3,3,1,64,128]{5,4,2,1,0,3:T(8,128)(2,1)S(1)}, u32[]{:S(2)}, u32[]{:S(2)}) collective-permute-start(bf16[1,3,3,1,64,128]{5,4,2,1,0,3:T(8,128)(2,1)S(1)} %bitcast.337), channel_id=1, source_target_pairs={{64,0},{128,64},{192,128},{256,192},{320,256},{384,320},{448,384},... | collective-permute-start | bytes 442376 | tf_op jit(solution)/shard_map/ppermute | solution.py:33
  296.1 7.5 %collective-permute-start.32 = (bf16[3,1,3,1,64,128]{5,4,2,1,0,3:T(8,128)(2,1)S(1)}, bf16[3,1,3,1,64,128]{5,4,2,1,0,3:T(8,128)(2,1)S(1)}, u32[]{:S(2)}, u32[]{:S(2)}) collective-permute-start(bf16[3,1,3,1,64,128]{5,4,2,1,0,3:T(8,128)(2,1)S(1)} %get-tuple-element.424), channel_id=1, source_target_pairs={{0,8},{8,16},{16,24},{24,32},{32,40},{40,48},{48,56},{56,0},{1,9},... | collective-permute-start | bytes 442376 | tf_op jit(solution)/shard_map/ppermute | solution.py:31
  305.2 7.2 %collective-permute-start.34 = (bf16[3,3,1,1,64,128]{5,4,2,1,0,3:T(8,128)(2,1)S(1)}, bf16[3,3,1,1,64,128]{5,4,2,1,0,3:T(8,128)(2,1)S(1)}, u32[]{:S(2)}, u32[]{:S(2)}) collective-permute-start(bf16[3,3,1,1,64,128]{5,4,2,1,0,3:T(8,128)(2,1)S(1)} %get-tuple-element.422), channel_id=1, source_target_pairs={{0,1},{1,2},{2,3},{3,4},{4,5},{5,6},{6,7},{7,0},{8,9},{9,10},{10,1... | collective-permute-start | bytes 442376 | tf_op jit(solution)/shard_map/ppermute | solution.py:31
  309.4 6.4 %collective-permute-start.35 = (bf16[3,3,1,1,64,128]{5,4,2,1,0,3:T(8,128)(2,1)S(1)}, bf16[3,3,1,1,64,128]{5,4,2,1,0,3:T(8,128)(2,1)S(1)}, u32[]{:S(2)}, u32[]{:S(2)}) collective-permute-start(bf16[3,3,1,1,64,128]{5,4,2,1,0,3:T(8,128)(2,1)S(1)} %get-tuple-element.423), channel_id=1, source_target_pairs={{1,0},{2,1},{3,2},{4,3},{5,4},{6,5},{7,6},{0,7},{9,8},{10,9},{11,1... | collective-permute-start | bytes 442376 | tf_op jit(solution)/shard_map/ppermute | solution.py:33
  553.9 9.9 %collective-permute-start.36 = (f32[1,3,3,1,192]{4,2,1,3,0:T(4,128)S(1)}, f32[1,3,3,1,192]{4,2,1,3,0:T(4,128)S(1)}, u32[]{:S(2)}, u32[]{:S(2)}) collective-permute-start(f32[1,3,3,1,192]{4,2,1,3,0:T(4,128)S(1)} %slice.502), channel_id=1, source_target_pairs={{0,64},{64,128},{128,192},{192,256},{256,320},{320,384},{384,448},... | collective-permute-start | bytes 20744 | tf_op jit(solution)/shard_map/ppermute | solution.py:31
  557.3 6.4 %collective-permute-start.37 = (f32[1,3,3,1,192]{4,2,1,0,3:T(4,128)S(1)}, f32[1,3,3,1,192]{4,2,1,0,3:T(4,128)S(1)}, u32[]{:S(2)}, u32[]{:S(2)}) collective-permute-start(f32[1,3,3,1,192]{4,2,1,0,3:T(4,128)S(1)} %bitcast.343), channel_id=1, source_target_pairs={{64,0},{128,64},{192,128},{256,192},{320,256},{384,320},{448,384},... | collective-permute-start | bytes 20744 | tf_op jit(solution)/shard_map/ppermute | solution.py:33
  563.8 5.8 %collective-permute-start.38 = (f32[3,1,3,1,192]{4,2,1,0,3:T(4,128)S(1)}, f32[3,1,3,1,192]{4,2,1,0,3:T(4,128)S(1)}, u32[]{:S(2)}, u32[]{:S(2)}) collective-permute-start(f32[3,1,3,1,192]{4,2,1,0,3:T(4,128)S(1)} %get-tuple-element.440), channel_id=1, source_target_pairs={{0,8},{8,16},{16,24},{24,32},{32,40},{40,48},{48,56},{56,0},{1,9},... | collective-permute-start | bytes 20744 | tf_op jit(solution)/shard_map/ppermute | solution.py:31
  569.7 7.4 %collective-permute-start.40 = (f32[3,3,1,1,192]{4,2,1,0,3:T(1,128)S(1)}, f32[3,3,1,1,192]{4,2,1,0,3:T(1,128)S(1)}, u32[]{:S(2)}, u32[]{:S(2)}) collective-permute-start(f32[3,3,1,1,192]{4,2,1,0,3:T(1,128)S(1)} %get-tuple-element.438), channel_id=1, source_target_pairs={{0,1},{1,2},{2,3},{3,4},{4,5},{5,6},{6,7},{7,0},{8,9},{9,10},{10,1... | collective-permute-start | bytes 20744 | tf_op jit(solution)/shard_map/ppermute | solution.py:31
  (199 other events, 856.7 us)
where the time goes:
time: 586 us; the launch traced here: 578 us
  other arithmetic  233 us (40%)
  local copies, waits for them, and re-layouts  154 us (26%)
  starting transfers between devices  130 us (22%)
  matrix products  29 us (5%)
  waiting for transfers between devices  20.2 us (3%)
  loops' own time  8.78 us (1%)
    scatter-add x32, other arithmetic, one_block(): totals = totals.at[targets].add(message)  83.2 us
    ppermute x21, starting transfers between devices, padded(): lax.ppermute(head, axis, [((i + 1) % count, i) for i in range(count)])  70.5 us
    ppermute x21, starting transfers between devices, padded(): lax.ppermute(tail, axis, [(i, (i + 1) % count) for i in range(count)])  59.7 us
    scatter-add x32, other arithmetic, one_block(): partial_value.at[targets].add(on_target).at[anchors].add(on_source)  58.3 us
    dot_general x116, matrix products, multiply(): return jnp.dot(left, right, preferred_element_type=jnp.float32)  28.8 us
    slice x32, local copies, waits for them, and re-layouts, one_block(): pair_list[1]  24.2 us
    gather x64, local copies, waits for them, and re-layouts, one_block(): source_places[targets]  18.4 us
    gather x64, local copies, waits for them, and re-layouts, one_block(): source_places[anchors]  18.4 us
  transfers between devices with their start and end apart: 42, of which 16 were waited for; matrix products, arithmetic and copies ran while one was open for 7% of the time, Pallas kernels for 0%

commit v1 on v0

--- a/solution.py
+++ b/solution.py
@@ -4,13 +4,20 @@
 import jax.numpy as jnp
 import numpy as np
 from jax import lax
+from jax.experimental import pallas as pl
+from jax.experimental.pallas import tpu as pltpu
 from jax.sharding import PartitionSpec as P
 
 NB = 8
 TILE = 64
 LAYERS = 2
 PAIR_BLOCK = 2
-
+LANES = 128
+GROUPS = NB // 2
+NEAR = 26
+CAP = 32
+AXES = ("gx", "gy", "gz")
+MESH = pl.DeviceIdType.MESH
 
 CUTOFF = 5.0
 BASIS_WIDTH = 0.6
@@ -19,6 +26,7 @@
 FAR_AWAY = 1000.0
 DEAD_SPACING = 100.0
 DENSITY = 0.1
+STEP = 4.2 / (NB - 1)
 
 
 def padded(cells, sides, width):
@@ -150,7 +158,7 @@
     return padded(bundle, (("gz", 2),), 1)[:, :, 0::2]
 
 
-def body(
+def whole_path(
     features,
     coords,
     counts,
@@ -253,6 +261,600 @@
     return (hidden_features.reshape(1, 1, 1, slot_count, channels), forces)
 
 
+VMEM = pl.BlockSpec(memory_space=pltpu.VMEM)
+SMEM = pl.BlockSpec(memory_space=pltpu.SMEM)
+
+
+def code_of(n):
+    return n + (1 if n >= 13 else 0)
+
+
+def exchange_kernel(shared, axis, kinds, *refs):
+    has_flag = axis is not None
+    blocks = refs[:kinds]
+    flag = refs[kinds] if has_flag else None
+    landed = refs[kinds + has_flag : 2 * kinds + has_flag]
+    rest = refs[2 * kinds + has_flag :]
+    flags = rest[0] if has_flag else None
+    rest = rest[has_flag:]
+    send, receive = rest[0], rest[1]
+    place = [lax.axis_index(name) for name in AXES]
+    size = [lax.axis_size(name) for name in AXES]
+
+    def beside(n):
+        code = code_of(n)
+        steps = (code // 9 - 1, code // 3 % 3 - 1, code % 3 - 1)
+        return tuple(
+            lax.rem(p + (step + s), s) if step else p for p, step, s in zip(place, steps, size)
+        )
+
+    def along(j):
+        return tuple(
+            lax.rem(p + j, s) if name == axis else p for p, name, s in zip(place, AXES, size)
+        )
+
+    count = size[AXES.index(axis)] if has_flag else 0
+    barrier = pltpu.get_barrier_semaphore()
+    for n in range(NEAR):
+        pl.semaphore_signal(barrier, inc=1, device_id=beside(n), device_id_type=MESH)
+    for j in range(1, count):
+        pl.semaphore_signal(barrier, inc=1, device_id=along(j), device_id_type=MESH)
+    pl.semaphore_wait(barrier, NEAR + max(count - 1, 0))
+
+    copies = []
+    for n in range(NEAR):
+        for kind in range(kinds):
+            copies.append(
+                pltpu.make_async_remote_copy(
+                    src_ref=blocks[kind].at[0 if shared else n],
+                    dst_ref=landed[kind].at[NEAR - 1 - n],
+                    send_sem=send.at[kind, n],
+                    recv_sem=receive.at[kind, NEAR - 1 - n],
+                    device_id=beside(n),
+                    device_id_type=MESH,
+                )
+            )
+    for j in range(1, count):
+        copies.append(
+            pltpu.make_async_remote_copy(
+                src_ref=flag,
+                dst_ref=flags.at[j],
+                send_sem=rest[2].at[j],
+                recv_sem=rest[3].at[j],
+                device_id=along(j),
+                device_id_type=MESH,
+            )
+        )
+    for copy in copies:
+        copy.start()
+    for copy in copies:
+        copy.wait()
+
+
+def exchange(identity, blocks, shared=False, flag=None, axis=None):
+    kinds = len(blocks)
+    shape = jax.ShapeDtypeStruct
+    outs = [shape((NEAR,) + b.shape[1:], b.dtype) for b in blocks]
+    scratch = [pltpu.SemaphoreType.DMA((kinds, NEAR)), pltpu.SemaphoreType.DMA((kinds, NEAR))]
+    operands = list(blocks)
+    if flag is not None:
+        around = lax.axis_size(axis)
+        outs.append(shape((around,) + flag.shape, flag.dtype))
+        scratch += [pltpu.SemaphoreType.DMA((around,)), pltpu.SemaphoreType.DMA((around,))]
+        operands.append(flag)
+
+    def kernel(*refs):
+        exchange_kernel(shared, axis, kinds, *refs)
+
+    return pl.pallas_call(
+        kernel,
+        name=f"exchange_{identity}",
+        out_shape=outs,
+        in_specs=[VMEM] * len(operands),
+        out_specs=[VMEM] * len(outs),
+        scratch_shapes=scratch,
+        compiler_params=pltpu.CompilerParams(collective_id=identity, has_side_effects=True),
+    )(*operands)
+
+
+def raised(own, flags):
+    found = own[...]
+    for j in range(1, flags.shape[0]):
+        found = jnp.maximum(found, flags[j])
+    return found
+
+
+def three_parts(values):
+    high = values.astype(jnp.bfloat16).astype(jnp.float32)
+    middle = (values - high).astype(jnp.bfloat16).astype(jnp.float32)
+    low = values - high - middle
+    return jnp.concatenate([high, middle, low], axis=0).astype(jnp.bfloat16)
+
+
+def joined(parts):
+    return parts[0:8] + parts[8:16] + parts[16:24]
+
+
+def across(left, right):
+    return lax.dot_general(left, right, (((1,), (1,)), ((), ())), preferred_element_type=jnp.float32)
+
+
+def iota(shape, dim):
+    return lax.broadcasted_iota(jnp.int32, shape, dim)
+
+
+def picked_start(coords, count):
+    slots = coords.shape[1]
+    slot = iota((3, slots), 1)
+    start = jnp.where(slot < count, coords[...], FAR_AWAY + DEAD_SPACING * slot.astype(jnp.float32))
+    return jnp.concatenate([start, jnp.zeros((5, slots), jnp.float32)], axis=0)
+
+
+def send_kernel(counts, lists, features, coords, rows_out, spots_out, flag_out, table):
+    slots = features.shape[0]
+    table[...] = jnp.zeros_like(table)
+    for n in range(NEAR):
+        for part in range(slots // LANES):
+            table[n : n + 1, part * LANES : (part + 1) * LANES] = lists[n, part : part + 1, :]
+    held = table[...]
+    row = iota(held.shape, 0)
+    code = row + jnp.where(row >= 13, 1, 0)
+    mine = jnp.logical_and(lax.shift_right_logical(held, 9) == 26 - code, row < NEAR)
+    slot = jnp.bitwise_and(held, 511).astype(jnp.float32)
+    before = (iota((slots, slots), 0) < iota((slots, slots), 1)).astype(jnp.float32)
+    chosen = jnp.where(mine, 1.0, 0.0)
+    rank = jnp.dot(
+        chosen.astype(jnp.bfloat16), before.astype(jnp.bfloat16), preferred_element_type=jnp.float32
+    )
+    rank = jnp.where(mine, rank, -1.0)
+    many = jnp.max(jnp.sum(chosen, axis=1, keepdims=True))
+    flag_out[...] = jnp.full((8, LANES), jnp.where(many > CAP, 1, 0), jnp.int32)
+    parts = three_parts(picked_start(coords, counts[0]))
+    order = iota((CAP, slots), 0).astype(jnp.float32)
+    lane = iota((CAP, slots), 1).astype(jnp.float32)
+    spots_out[...] = jnp.zeros_like(spots_out)
+    for n in range(NEAR):
+        hit = rank[n : n + 1, :] == order
+        place = jnp.sum(jnp.where(hit, slot[n : n + 1, :], 0.0), axis=1, keepdims=True)
+        select = (place == lane).astype(jnp.float32).astype(jnp.bfloat16)
+        rows_out[n] = jnp.dot(select, features[...], preferred_element_type=jnp.float32).astype(
+            jnp.bfloat16
+        )
+        spots_out[n, :, 0:CAP] = joined(across(parts, select))
+
+
+def take_kernel(
+    edge,
+    counts,
+    list_block,
+    lists,
+    features,
+    coords,
+    rows_in,
+    spots_in,
+    flag_in,
+    flags,
+    lift,
+    hidden_out,
+    rows_out,
+    spots_out,
+    asked_rows,
+    asked_spots,
+    wants_out,
+    flag_out,
+    gathered,
+    beside,
+    select,
+    ready,
+):
+    slots, channels = features.shape
+    tiles = slots // TILE
+    own_base = gathered.shape[0] - slots
+    bring = pltpu.make_async_copy(lists.at[:, 4, :], wants_out, ready)
+    bring.start()
+    flag_out[...] = raised(flag_in, flags)
+    row_parts = [list_block[0, part : part + 1, :] for part in range(slots // LANES)]
+    row_all = jnp.concatenate(row_parts, axis=1)
+    code_row = lax.shift_right_logical(row_all, 9)
+    code_row_f = code_row.astype(jnp.float32)
+    for first in range(slots // LANES):
+        turned = jnp.transpose(
+            jnp.broadcast_to(row_parts[first].astype(jnp.float32), (LANES, LANES))
+        ).astype(jnp.int32)
+        code = lax.shift_right_logical(turned, 9)
+        slot = jnp.bitwise_and(turned, 511)
+        code_f = code.astype(jnp.float32)
+        total = jnp.zeros((LANES, LANES), jnp.float32)
+        level = iota((LANES, LANES), 0)
+        lane = iota((LANES, LANES), 1)
+        for second in range(first + 1):
+            same = code_f == code_row_f[:, second * LANES : (second + 1) * LANES]
+            if second == first:
+                same = jnp.logical_and(same, lane < level)
+            total = total + jnp.where(same, 1.0, 0.0)
+        rank = jnp.sum(total, axis=1, keepdims=True).astype(jnp.int32)
+        neighbour = code - jnp.where(code >= 13, 1, 0)
+        index = jnp.where(code == 13, own_base + slot, neighbour * CAP + rank)
+        for block in range(gathered.shape[0] // LANES):
+            hit = index == lane + block * LANES
+            select[first * LANES : (first + 1) * LANES, block * LANES : (block + 1) * LANES] = (
+                jnp.where(hit, 1.0, 0.0).astype(jnp.bfloat16)
+            )
+    taken = NEAR * CAP
+    gathered[0:taken, :] = rows_in[...].reshape(taken, channels)
+    gathered[taken:own_base, :] = jnp.zeros((own_base - taken, channels), jnp.bfloat16)
+    gathered[own_base:, :] = features[...]
+    beside[:, 0:own_base] = jnp.zeros((8, own_base), jnp.float32)
+    for n in range(NEAR):
+        beside[:, n * CAP : (n + 1) * CAP] = spots_in[n, :, 0:CAP]
+    beside[:, own_base:] = picked_start(coords, counts[0])
+    hidden = jnp.dot(select[...], gathered[...], preferred_element_type=jnp.float32).astype(jnp.bfloat16)
+    hidden_out[...] = hidden.reshape(hidden_out.shape)
+    projected = jnp.dot(hidden, lift[...], preferred_element_type=jnp.float32).astype(jnp.bfloat16)
+    rows_out[...] = projected.reshape(rows_out.shape)
+    placed = joined(across(three_parts(beside[...]), select[...]))
+    high = jnp.where(code_row >= 9, 1, 0) + jnp.where(code_row >= 18, 1, 0)
+    rest = code_row - 9 * high
+    middle = jnp.where(rest >= 3, 1, 0) + jnp.where(rest >= 6, 1, 0)
+    low = rest - 3 * middle
+    line = iota((8, slots), 0)
+    shift = jnp.where(line == 0, high - 1, jnp.where(line == 1, middle - 1, low - 1))
+    placed = placed + shift.astype(jnp.float32) * edge
+    half = iota((8, LANES), 1) < TILE
+    for t in range(tiles):
+        part = placed[:, t // 2 * LANES : (t // 2 + 1) * LANES]
+        swapped = pltpu.roll(part, TILE, 1)
+        spots_out[t] = jnp.where(half, part, swapped) if t % 2 == 0 else jnp.where(half, swapped, part)
+    bring.wait()
+    for n in range(NEAR):
+        reader = 26 - code_of(n)
+        asked_rows[n] = rows_out[wants_out[n, reader]]
+        near = spots_out[wants_out[n, reader]]
+        later = pltpu.roll(spots_out[wants_out[n, 32 + reader]], 3, 0)
+        asked_spots[n] = jnp.where(iota((8, LANES), 0) < 3, near, later)
+
+
+def layer_kernel(with_force, edge, pairs, force_weight, wants, own_rows, near_rows, own_spots, near_spots, *refs):
+    if with_force:
+        (hidden, radial, mix, out_weight, flag_in, flags) = refs[:6]
+        (renewed, own_force, near_force, flag_out) = refs[6:10]
+        (rows, spots, totals, wide, edges, weighted, on_target, on_source) = refs[10:]
+    else:
+        (hidden, radial, mix, out_weight, flag_in, flags, lift) = refs[:7]
+        (renewed, projected, asked, flag_out) = refs[7:11]
+        (rows, spots, totals, wide, edges, weighted) = refs[11:]
+    tiles = hidden.shape[0]
+    channels = rows.shape[2]
+    flag_out[...] = raised(flag_in, flags)
+    half = iota((TILE, LANES), 1) // TILE
+    within = iota((TILE, LANES), 1) % TILE
+    eye = (within == iota((TILE, LANES), 0)).astype(jnp.float32)
+    upper = half.astype(jnp.float32)
+    totals[...] = jnp.zeros_like(totals)
+    rows[0:tiles] = own_rows[...]
+    spots[0:tiles] = own_spots[...]
+    rows[tiles + 13] = jnp.zeros(rows.shape[1:], rows.dtype)
+    spots[tiles + 13] = jnp.zeros(spots.shape[1:], spots.dtype)
+    for n in range(NEAR):
+        code = code_of(n)
+        rows[tiles + code] = near_rows[n]
+        steps = (code // 9 - 1, code // 3 % 3 - 1, code % 3 - 1)
+        for axis in range(3):
+            line = axis + (3 if with_force else 0)
+            spots[tiles + code, axis : axis + 1, :] = near_spots[n, line : line + 1, :] + steps[axis] * edge
+    if with_force:
+        on_target[...] = jnp.zeros_like(on_target)
+        on_source[...] = jnp.zeros_like(on_source)
+    for t in range(tiles):
+        turned = jnp.transpose(jnp.broadcast_to(spots[t][None], (16, 8, LANES)).reshape(LANES, LANES))
+        for axis in range(3):
+            wide[t, axis] = jnp.broadcast_to(turned[:TILE, axis : axis + 1], (TILE, LANES))
+
+    def one_pair(pair, slot):
+        target = pairs[0, pair]
+        source = pairs[1, pair]
+        same = jnp.where(target == source, 1.0, 0.0).astype(jnp.float32)
+        spot = spots[source]
+        gap = [wide[target, axis] - spot[axis : axis + 1, :] for axis in range(3)]
+        square = gap[0] * gap[0] + gap[1] * gap[1] + gap[2] * gap[2] + SOFTENING
+        inverse = lax.rsqrt(square)
+        distance = square * inverse
+        ramp = 1.0 - jnp.minimum(square * (1.0 / (CUTOFF * CUTOFF)), 1.0)
+        envelope = ramp * ramp * (1.0 - same * eye)
+        unit = [g * inverse for g in gap]
+        scaled = (distance - (0.5 + STEP * upper)) * (1.0 / BASIS_WIDTH)
+        root_three = math.sqrt(3.0)
+        root_five = math.sqrt(5.0)
+        root_fifteen = math.sqrt(15.0)
+        fifteen = [root_fifteen * u for u in unit]
+        angular = [
+            None,
+            root_three * unit[0],
+            root_three * unit[1],
+            root_three * unit[2],
+            fifteen[0] * unit[1],
+            fifteen[1] * unit[2],
+            (1.5 * root_five) * unit[2] * unit[2] - 0.5 * root_five,
+            fifteen[0] * unit[2],
+            0.5 * (fifteen[0] * unit[0] - fifteen[1] * unit[1]),
+        ]
+        profile = None
+        for q in range(GROUPS):
+            moved = scaled - (2.0 * q * STEP / BASIS_WIDTH)
+            basis = jnp.exp(-(moved * moved)) * envelope
+            if with_force:
+                weight = jnp.where(half == 0, force_weight[2 * q], force_weight[2 * q + 1])
+                profile = weight * basis if profile is None else profile + weight * basis
+            columns = slice(q * LANES, (q + 1) * LANES)
+            edges[slot, 0:TILE, columns] = basis.astype(jnp.bfloat16)
+            for m in range(1, 9):
+                edges[slot, m * TILE : (m + 1) * TILE, columns] = (angular[m] * basis).astype(jnp.bfloat16)
+        near = rows[source]
+        full = near.astype(jnp.float32)
+        for k in range(3 * NB):
+            weighted[slot, k // NB, (k % NB) * TILE : (k % NB + 1) * TILE, :] = (
+                full * radial[k : k + 1, :]
+            ).astype(jnp.bfloat16)
+        for order, (low, high) in enumerate(((0, 1), (1, 4), (4, 9))):
+            message = multiply(edges[slot, low * TILE : high * TILE, :], weighted[slot, order])
+            totals[target, low * TILE : high * TILE, :] += message
+        if with_force:
+            twice = jnp.concatenate([near, near], axis=0)
+            strength = profile * across(rows[target], twice)
+            for axis in range(3):
+                push = strength * unit[axis]
+                on_target[target, axis] += push
+                on_source[source, axis] += jnp.sum(push.reshape(TILE // 8, 8, LANES), axis=0)
+
+    count = pairs.shape[1]
+
+    def two_pairs(step, carried):
+        one_pair(2 * step, 0)
+        one_pair(2 * step + 1, 1)
+        return carried
+
+    lax.fori_loop(0, count // 2, two_pairs, 0)
+    for left in range(count // 2 * 2, count):
+        one_pair(left, 0)
+
+    def one_tile(t, carried):
+        def part(m):
+            return totals[t, m * TILE : (m + 1) * TILE, :] * MESSAGE_SCALE
+
+        vector = part(1) ** 2 + part(2) ** 2 + part(3) ** 2
+        tensor = part(4) ** 2 + part(5) ** 2 + part(6) ** 2 + part(7) ** 2 + part(8) ** 2
+        mixed = mix[0:1, :] * part(0) + mix[1:2, :] * vector + mix[2:3, :] * tensor
+        active = (mixed / (1.0 + jnp.exp(-mixed))).astype(jnp.bfloat16)
+        fresh = (hidden[t].astype(jnp.float32) + multiply(active, out_weight[...])).astype(jnp.bfloat16)
+        renewed[t] = fresh
+        if not with_force:
+            projected[t] = multiply(fresh, lift[...]).astype(jnp.bfloat16)
+        return carried
+
+    lax.fori_loop(0, tiles, one_tile, 0)
+    if not with_force:
+        for n in range(NEAR):
+            asked[n] = projected[wants[n, 32 + 26 - code_of(n)]]
+    else:
+        factor = 0.5 / math.sqrt(channels)
+        lane = iota((TILE, LANES), 1)
+        line = iota((8, LANES), 0)
+
+        def folded(b):
+            sums = jnp.zeros((8, LANES), jnp.float32)
+            for axis in range(3):
+                summed = jnp.sum(on_source[b, axis], axis=0, keepdims=True)
+                sums = jnp.where(line == axis, jnp.broadcast_to(summed, (8, LANES)), sums)
+            return (sums + pltpu.roll(sums, TILE, 1)) * factor
+
+        for t in range(tiles):
+            columns = jnp.zeros((TILE, LANES), jnp.float32)
+            for axis in range(3):
+                summed = jnp.sum(on_target[t, axis], axis=1, keepdims=True)
+                columns = jnp.where(lane == axis, summed, columns)
+            turned = jnp.transpose(jnp.concatenate([columns, columns], axis=0))[0:8, :]
+            own_force[t] = turned * factor - folded(t)
+        for n in range(NEAR):
+            near_force[n] = -folded(tiles + code_of(n))
+
+
+def force_kernel(wants, own_force, arrived, forces, total):
+    total[...] = own_force[...]
+    for n in range(NEAR):
+        tile = wants[n, 32 + 26 - code_of(n)]
+        total[tile] += arrived[n]
+    half = iota((8, LANES), 1) < TILE
+    for block in range(total.shape[0] // 2):
+        both = jnp.where(half, total[2 * block], total[2 * block + 1])
+        forces[:, block * LANES : (block + 1) * LANES] = both[0:3, :]
+
+
+def call(kernel, name, out_shape, in_specs, out_specs, scratch, operands):
+    return pl.pallas_call(
+        kernel,
+        name=name,
+        out_shape=out_shape,
+        in_specs=in_specs,
+        out_specs=out_specs,
+        scratch_shapes=scratch,
+        compiler_params=pltpu.CompilerParams(vmem_limit_bytes=40 * 1024 * 1024),
+    )(*operands)
+
+
+def body(
+    features,
+    coords,
+    counts,
+    sources,
+    wanted,
+    pairs,
+    lifting_weight,
+    radial_weight,
+    mix_weight,
+    out_weight,
+    force_weight,
+):
+    slots, channels = features.shape[3], features.shape[4]
+    tiles = slots // TILE
+    edge = float((slots / DENSITY) ** (1.0 / 3.0))
+    shape = jax.ShapeDtypeStruct
+    flat_features = features.reshape(slots, channels)
+    flat_coords = coords.reshape(3, slots)
+    flat_counts = counts.reshape(1)
+    pair_list = pairs.reshape(2, pairs.shape[4])
+    wants = jnp.pad(wanted.reshape(LAYERS, 27), ((0, 0), (0, 5))).reshape(1, LAYERS * 32)
+    list_block = jnp.concatenate(
+        [
+            sources.reshape(slots // LANES, LANES),
+            jnp.pad(wants, ((0, 3), (0, LANES - LAYERS * 32))),
+        ],
+        axis=0,
+    )[None]
+    (lists,) = exchange(1, [list_block], shared=True)
+    tile_shape = shape((tiles, TILE, channels), jnp.bfloat16)
+    spot_shape = shape((tiles, 8, LANES), jnp.float32)
+    near_tiles = shape((NEAR, TILE, channels), jnp.bfloat16)
+    near_spots = shape((NEAR, 8, LANES), jnp.float32)
+    flag_shape = shape((8, LANES), jnp.int32)
+    moved_rows, moved_spots, flag = call(
+        send_kernel,
+        "send_rows",
+        [shape((NEAR, CAP, channels), jnp.bfloat16), near_spots, flag_shape],
+        [SMEM, VMEM, VMEM, VMEM],
+        [VMEM] * 3,
+        [pltpu.VMEM((32, slots), jnp.int32)],
+        (flat_counts, lists, flat_features, flat_coords),
+    )
+    rows_in, spots_in, flags = exchange(2, [moved_rows, moved_spots], flag=flag, axis="gx")
+    held = -(-NEAR * CAP // LANES) * LANES + slots
+
+    def take(*refs):
+        take_kernel(edge, *refs)
+
+    hidden, own_rows, own_spots, asked_rows, asked_spots, wants_list, flag = call(
+        take,
+        "take_rows",
+        [tile_shape, tile_shape, spot_shape, near_tiles, near_spots, shape((NEAR, LANES), jnp.int32), flag_shape],
+        [SMEM] + [VMEM] * 9,
+        [VMEM] * 5 + [SMEM, VMEM],
+        [
+            pltpu.VMEM((held, channels), jnp.bfloat16),
+            pltpu.VMEM((8, held), jnp.float32),
+            pltpu.VMEM((slots, held), jnp.bfloat16),
+            pltpu.SemaphoreType.DMA,
+        ],
+        (
+            flat_counts,
+            list_block,
+            lists,
+            flat_features,
+            flat_coords,
+            rows_in,
+            spots_in,
+            flag,
+            flags,
+            lifting_weight[0],
+        ),
+    )
+    near_rows, near_places, flags = exchange(3, [asked_rows, asked_spots], flag=flag, axis="gy")
+    scratch = [
+        pltpu.VMEM((tiles + 27, TILE, channels), jnp.bfloat16),
+        pltpu.VMEM((tiles + 27, 8, LANES), jnp.float32),
+        pltpu.VMEM((tiles, 9 * TILE, channels), jnp.float32),
+        pltpu.VMEM((tiles, 3, TILE, LANES), jnp.float32),
+        pltpu.VMEM((2, 9 * TILE, NB * TILE), jnp.bfloat16),
+        pltpu.VMEM((2, 3, NB * TILE, channels), jnp.bfloat16),
+    ]
+
+    def first(*refs):
+        layer_kernel(False, edge, *refs)
+
+    def last(*refs):
+        layer_kernel(True, edge, *refs)
+
+    hidden, own_rows, asked_rows, flag = call(
+        first,
+        "layer_first",
+        [tile_shape, tile_shape, near_tiles, flag_shape],
+        [SMEM] * 3 + [VMEM] * 11,
+        [VMEM] * 4,
+        scratch,
+        (
+            pair_list,
+            force_weight,
+            wants_list,
+            own_rows,
+            near_rows,
+            own_spots,
+            near_places,
+            hidden,
+            radial_weight[0].reshape(3 * NB, channels),
+            mix_weight[0],
+            out_weight[0],
+            flag,
+            flags,
+            lifting_weight[1],
+        ),
+    )
+    near_rows, flags = exchange(4, [asked_rows], flag=flag, axis="gz")
+    updated, own_force, near_force, flag = call(
+        last,
+        "layer_last",
+        [tile_shape, spot_shape, near_spots, flag_shape],
+        [SMEM] * 3 + [VMEM] * 10,
+        [VMEM] * 4,
+        scratch
+        + [
+            pltpu.VMEM((tiles, 3, TILE, LANES), jnp.float32),
+            pltpu.VMEM((tiles + 27, 3, 8, LANES), jnp.float32),
+        ],
+        (
+            pair_list,
+            force_weight,
+            wants_list,
+            own_rows,
+            near_rows,
+            own_spots,
+            near_places,
+            hidden,
+            radial_weight[1].reshape(3 * NB, channels),
+            mix_weight[1],
+            out_weight[1],
+            flag,
+            flags,
+        ),
+    )
+    (arrived,) = exchange(5, [near_force])
+    (forces,) = call(
+        force_kernel,
+        "add_forces",
+        [shape((3, slots), jnp.float32)],
+        [SMEM, VMEM, VMEM],
+        [VMEM],
+        [pltpu.VMEM((tiles, 8, LANES), jnp.float32)],
+        (wants_list, own_force, arrived),
+    )
+    updated = updated.reshape(features.shape)
+    forces = forces.reshape(coords.shape)
+    return lax.cond(
+        flag[0, 0] > 0,
+        lambda: whole_path(
+            features,
+            coords,
+            counts,
+            sources,
+            wanted,
+            pairs,
+            lifting_weight,
+            radial_weight,
+            mix_weight,
+            out_weight,
+            force_weight,
+        ),
+        lambda: (updated, forces),
+    )
+
+
 def solution(mesh):
     placed = (
         P("gx", "gy", "gz", None, None),

time: 586 us -> 141 us (0.24); the launches traced: 578 us -> 140 us
  other arithmetic: 233 us -> 1.28 us
  starting transfers between devices: 130 us -> 0 us
  local copies, waits for them, and re-layouts: 154 us -> 24.2 us
  Pallas kernels: 0 us -> 112 us
  matrix products: 29 us -> 0 us
  waiting for transfers between devices: 20.2 us -> 0 us
  loops' own time: 8.78 us -> 0.01 us
    scatter-add x64 -> x0, other arithmetic: 142 us -> none  [the longest x32 83.2 us: one_block(): totals = totals.at[targets].add(message)]
    ppermute x42 -> x0, starting transfers between devices: 130 us -> none  [the longest x21 70.5 us: padded(): lax.ppermute(head, axis, [((i + 1) % count, i) for i in range(count)])]
    pallas_call x0 -> x10, Pallas kernels: none -> 112 us  [the longest x5 74.6 us: exchange(): pl.pallas_call(kernel, name=f'exchange_{identity}', out_shape=outs, in_sp...]
    gather x183 -> x0, local copies, waits for them, and re-layouts: 72.8 us -> none  [the longest x64 18.4 us: one_block(): source_places[targets]]
    slice x188 -> x2, local copies, waits for them, and re-layouts: 34.3 us -> 1.28 us  [the longest x1 0.77 us: body(): mix_weight[1]]
    dot_general x117 -> x0, matrix products: 29 us -> none  [the longest x116 28.8 us: multiply(): return jnp.dot(left, right, preferred_element_type=jnp.float32)]
    convert_element_type x130 -> x0, other arithmetic: 20.9 us -> none  [the longest x32 11.9 us: pair_terms(): edges = (angular * basis[None]).astype(jnp.bfloat16)]
    ppermute x42 -> x0, waiting for transfers between devices: 20.2 us -> none  [the longest x21 16.1 us: padded(): lax.ppermute(head, axis, [((i + 1) % count, i) for i in range(count)])]
  transfers between devices with their start and end apart: 42 -> 0, of which waited for: 16 -> 0; matrix products, arithmetic and copies ran while one was open for 7% -> 0% of each run, Pallas kernels for 0% -> 0%
where the time goes in v1:
time: 141 us; the launch traced here: 140 us
  Pallas kernels  112 us (79%)
  local copies, waits for them, and re-layouts  24.2 us (17%)
  between operations  2.18 us (2%)
    pallas_call x5, Pallas kernels, exchange(): pl.pallas_call(kernel, name=f'exchange_{identity}', out_shape=outs, in_sp...  74.6 us
    pallas_call x5, Pallas kernels, call(): pl.pallas_call(kernel, name=name, out_shape=out_shape, in_specs=in_specs,...  37.8 us
    unnamed x67, local copies, waits for them, and re-layouts  20 us

profile of v1, /device:TPU:1, one launch (start us, length us, event | category | flops | bytes accessed | tf_op | source)
XLA Modules:
  0.0 140.0 jit_solution(2125004038805715870)
XLA Ops:
  0.7 0.7 pad.8
  1.4 1.3 fusion.59.refs_0_.refs_1_
  2.7 20.5 %exchange_1.1.lists.refs_2_ = s32[26,8,128]{2,1,0:T(8,128)} custom-call(s32[1,8,128]{2,1,0:T(8,128)} %fusion.59.refs_0_.refs_1_), custom_call_target="tpu_custom_call" | custom-call | tf_op jit(solution)/shard_map/exchange_1/pallas_call | solution.py:349
  23.2 0.7 copy.204
  24.5 0.9 copy-done
  25.4 2.0 %send_rows.1 = (bf16[26,32,128]{2,1,0:T(8,128)(2,1)S(1)}, f32[26,8,128]{2,1,0:T(8,128)S(1)}, s32[8,128]{1,0:T(8,128)S(1)}) custom-call(s32[1]{0:T(128)} %bitcast.333.counts, s32[26,8,128]{2,1,0:T(8,128)S(1)} %copy-done, bf16[512,128]{1,0:T(8,128)(2,1)} %bitcast.359, f32[3,512]{1,0:T(4,128)S(1)} %bitcast.335), custom_call_target="tpu_custom_call" | custom-call | tf_op jit(solution)/shard_map/send_rows/pallas_call | solution.py:673
  29.4 13.2 %exchange_2.1 = (bf16[26,32,128]{2,1,0:T(8,128)(2,1)}, f32[26,8,128]{2,1,0:T(8,128)}, s32[8,8,128]{2,1,0:T(8,128)}) custom-call(bf16[26,32,128]{2,1,0:T(8,128)(2,1)} %copy-done.9, f32[26,8,128]{2,1,0:T(8,128)} %copy-done.11, s32[8,128]{1,0:T(8,128)} %copy-done.23), custom_call_target="tpu_custom_call" | custom-call | tf_op jit(solution)/shard_map/exchange_2/pallas_call | solution.py:349
  42.7 0.8 slice_bitcast_fusion.23
  43.5 0.9 copy-done.1
  44.4 0.9 copy-done.10
  45.3 0.9 copy-done.12
  46.2 0.7 copy-done.15
  46.9 0.8 copy-done.17
  48.3 4.1 %take_rows.1 = (bf16[8,64,128]{2,1,0:T(8,128)(2,1)S(1)}, bf16[8,64,128]{2,1,0:T(8,128)(2,1)S(1)}, f32[8,8,128]{2,1,0:T(8,128)S(1)}, bf16[26,64,128]{2,1,0:T(8,12...) custom-call(s32[1]{0:T(128)} %bitcast.334.refs_0_, ...), custom_call_target="tpu_custom_call" | custom-call | tf_op jit(solution)/shard_map/take_rows/pallas_call | solution.py:673
  52.4 0.8 copy-done.4
  54.4 15.7 %exchange_3.1 = (bf16[26,64,128]{2,1,0:T(8,128)(2,1)}, f32[26,8,128]{2,1,0:T(8,128)}, s32[8,8,128]{2,1,0:T(8,128)}) custom-call(bf16[26,64,128]{2,1,0:T(8,128)(2,1)} %copy-done.4, f32[26,8,128]{2,1,0:T(8,128)} %copy-done.13, s32[8,128]{1,0:T(8,128)} %copy-done.19), custom_call_target="tpu_custom_call" | custom-call | tf_op jit(solution)/shard_map/exchange_3/pallas_call | solution.py:349
  70.1 0.8 fusion.74
  70.9 0.7 slice_bitcast_fusion.27
  71.6 1.0 copy-done.3
  72.6 0.9 copy-done.7
  73.5 0.8 copy-done.16
  74.3 0.7 copy-done.20
  74.9 15.4 %layer_first.1 = (bf16[8,64,128]{2,1,0:T(8,128)(2,1)S(1)}, bf16[8,64,128]{2,1,0:T(8,128)(2,1)S(1)}, bf16[26,64,128]{2,1,0:T(8,128)(2,1)S(1)}, s32[8,128]{1,0:T(8,128)S(1)}) custom-call(s32[2,32]{1,0:T(2,128)} %bitcast.373, f32[8]{0:T(128)} %refs_1_.3, s32[26,128]{1,0:T(8,128)S(1)} %get-tuple-element.435.refs_2_.wants, ...), custom_call_target="tpu_custom_call" | custom-call | tf_op jit(solution)/shard_map/layer_first/pallas_call | solution.py:673
  90.3 0.8 copy-done.6
  91.7 13.9 %exchange_4.1 = (bf16[26,64,128]{2,1,0:T(8,128)(2,1)}, s32[8,8,128]{2,1,0:T(8,128)}) custom-call(bf16[26,64,128]{2,1,0:T(8,128)(2,1)} %copy-done.6, s32[8,128]{1,0:T(8,128)} %copy-done.21), custom_call_target="tpu_custom_call" | custom-call | tf_op jit(solution)/shard_map/exchange_4/pallas_call | solution.py:349
  105.7 1.0 copy-done.5
  106.7 0.9 copy-done.8
  107.6 0.8 copy-done.18
  109.0 15.4 %layer_last.1 = (bf16[8,64,128]{2,1,0:T(8,128)(2,1)}, f32[8,8,128]{2,1,0:T(8,128)S(1)}, f32[26,8,128]{2,1,0:T(8,128)S(1)}, s32[8,128]{1,0:T(8,128)S(1)}) custom-call(s32[2,32]{1,0:T(2,128)S(1)} %bitcast.374, f32[8]{0:T(128)S(1)} %copy-done.57, s32[26,128]{1,0:T(8,128)S(1)} %get-tuple-element.435.refs_2_.wants, ...), custom_call_target="tpu_custom_call" | custom-call | tf_op jit(solution)/shard_map/layer_last/pallas_call | solution.py:673
  125.1 11.3 %exchange_5.1.arrived = f32[26,8,128]{2,1,0:T(8,128)} custom-call(f32[26,8,128]{2,1,0:T(8,128)} %copy-done.14), custom_call_target="tpu_custom_call" | custom-call | tf_op jit(solution)/shard_map/exchange_5/pallas_call | solution.py:349
  136.4 0.9 copy-done.2
  137.3 0.9 add_forces.1
  (55 shorter events, 7.6 us)
Async XLA Ops:
  0.6 105.0 %copy-start.41 = (s32[1,1,1,2,32]{4,3,2,1,0:T(2,128)S(1)}, s32[1,1,1,2,32]{4,3,2,1,0:T(2,128)}, u32[]{:S(2)}) copy-start(s32[1,1,1,2,32]{4,3,2,1,0:T(2,128)} %param.27) | copy-start | bytes 772
  0.6 105.0 %copy-start.57 = (f32[8]{0:T(128)S(1)}, f32[8]{0:T(128)}, u32[]{:S(2)}) copy-start(f32[8]{0:T(128)} %refs_1_.3) | copy-start | bytes 100
  24.5 0.9 copy-start
  27.5 0.7 copy-start.9
  28.2 0.6 copy-start.11
  29.4 110.0 %copy-start.31 = (bf16[1,1,1,512,128]{4,3,2,1,0:T(8,128)(2,1)S(1)}, bf16[1,1,1,512,128]{4,3,2,1,0:T(8,128)(2,1)}, u32[]{:S(2)}) copy-start(bf16[1,1,1,512,128]{4,3,2,1,0:T(8,128)(2,1)} %param.22) | copy-start | bytes 393220
  29.4 110.0 %copy-start.48 = (f32[2,3,8,128]{3,2,1,0:T(8,128)S(1)}, f32[2,3,8,128]{3,2,1,0:T(8,128)}, u32[]{:S(2)}) copy-start(f32[2,3,8,128]{3,2,1,0:T(8,128)} %param.29) | copy-start | bytes 73732
  29.4 110.0 %copy-start.55 = (s32[1,1,1,512]{3,2,1,0:T(1,128)S(1)}, s32[1,1,1,512]{3,2,1,0:T(1,128)}, u32[]{:S(2)}) copy-start(s32[1,1,1,512]{3,2,1,0:T(1,128)} %param.25) | copy-start | bytes 6148
  29.4 110.0 %copy-start.56 = (s32[1,1,1,2,27,1]{4,5,3,2,1,0:T(1,128)S(1)}, s32[1,1,1,2,27,1]{4,5,3,2,1,0:T(1,128)}, u32[]{:S(2)}) copy-start(s32[1,1,1,2,27,1]{4,5,3,2,1,0:T(1,128)} %param.26) | copy-start | bytes 652
  29.4 110.0 %copy-start.60 = (f32[1,1,1,3,512]{4,2,3,1,0:T(1,128)S(1)}, f32[1,1,1,3,512]{4,2,3,1,0:T(1,128)}, u32[]{:S(2)}) copy-start(f32[1,1,1,3,512]{4,2,3,1,0:T(1,128)} %param.23) | copy-start | bytes 18436
  29.4 110.0 %copy-start.62 = (f32[2,3,128]{2,0,1:T(2,128)S(1)}, f32[2,3,128]{2,0,1:T(2,128)}, u32[]{:S(2)}) copy-start(f32[2,3,128]{2,0,1:T(2,128)} %param.30) | copy-start | bytes 9220
  43.5 0.9 copy-start.1
  44.4 0.9 copy-start.10
  45.3 0.9 copy-start.12
  46.2 0.7 copy-start.15
  46.9 0.8 copy-start.17
  47.7 0.7 copy-start.24
  52.4 0.8 copy-start.4
  53.2 0.6 copy-start.13
  53.8 0.6 copy-start.19
  71.6 1.0 copy-start.3
  72.6 0.9 copy-start.7
  73.5 0.8 copy-start.16
  74.3 0.7 copy-start.20
  90.3 0.8 copy-start.6
  91.1 0.6 copy-start.21
  105.7 1.0 copy-start.5
  106.7 0.9 copy-start.8
  107.6 0.8 copy-start.18
  108.3 0.7 copy-start.22
  124.5 0.6 copy-start.14
  136.4 0.9 copy-start.2
  (1 other events, 0.6 us)

commit v2 on v0

--- a/solution.py
+++ b/solution.py
@@ -4,13 +4,20 @@
 import jax.numpy as jnp
 import numpy as np
 from jax import lax
+from jax.experimental import pallas as pl
+from jax.experimental.pallas import tpu as pltpu
 from jax.sharding import PartitionSpec as P
 
 NB = 8
 TILE = 64
 LAYERS = 2
 PAIR_BLOCK = 2
-
+LANES = 128
+GROUPS = NB // 2
+NEAR = 26
+CAP = 32
+AXES = ("gx", "gy", "gz")
+MESH = pl.DeviceIdType.MESH
 
 CUTOFF = 5.0
 BASIS_WIDTH = 0.6
@@ -19,6 +26,7 @@
 FAR_AWAY = 1000.0
 DEAD_SPACING = 100.0
 DENSITY = 0.1
+STEP = 4.2 / (NB - 1)
 
 
 def padded(cells, sides, width):
@@ -150,7 +158,7 @@
     return padded(bundle, (("gz", 2),), 1)[:, :, 0::2]
 
 
-def body(
+def whole_path(
     features,
     coords,
     counts,
@@ -253,6 +261,579 @@
     return (hidden_features.reshape(1, 1, 1, slot_count, channels), forces)
 
 
+VMEM = pl.BlockSpec(memory_space=pltpu.VMEM)
+SMEM = pl.BlockSpec(memory_space=pltpu.SMEM)
+ANY = pl.BlockSpec(memory_space=pl.ANY)
+
+
+def code_of(n):
+    return n + (1 if n >= 13 else 0)
+
+
+def steps_of(code):
+    return (code // 9 - 1, code // 3 % 3 - 1, code % 3 - 1)
+
+
+def beside(n):
+    found = []
+    for name, step in zip(AXES, steps_of(code_of(n))):
+        place, size = lax.axis_index(name), lax.axis_size(name)
+        found.append(lax.rem(place + (step + size), size) if step else place)
+    return tuple(found)
+
+
+def started(neighbours, source_of, target_of, send, receive):
+    copies = []
+    for n in range(NEAR):
+        copy = pltpu.make_async_remote_copy(
+            src_ref=source_of(n),
+            dst_ref=target_of(NEAR - 1 - n),
+            send_sem=send.at[n],
+            recv_sem=receive.at[NEAR - 1 - n],
+            device_id=neighbours[n],
+            device_id_type=MESH,
+        )
+        copy.start()
+        copies.append(copy)
+    return copies
+
+
+def finish(copies):
+    for copy in copies:
+        copy.wait()
+
+
+def three_parts(values):
+    high = values.astype(jnp.bfloat16).astype(jnp.float32)
+    middle = (values - high).astype(jnp.bfloat16).astype(jnp.float32)
+    low = values - high - middle
+    return jnp.concatenate([high, middle, low], axis=0).astype(jnp.bfloat16)
+
+
+def joined(parts):
+    return parts[0:8] + parts[8:16] + parts[16:24]
+
+
+def across(left, right):
+    return lax.dot_general(left, right, (((1,), (1,)), ((), ())), preferred_element_type=jnp.float32)
+
+
+def iota(shape, dim):
+    return lax.broadcasted_iota(jnp.int32, shape, dim)
+
+
+def picked_start(coords, count):
+    slots = coords.shape[1]
+    slot = iota((3, slots), 1)
+    start = jnp.where(slot < count, coords[...], FAR_AWAY + DEAD_SPACING * slot.astype(jnp.float32))
+    return jnp.concatenate([start, jnp.zeros((5, slots), jnp.float32)], axis=0)
+
+
+def pair_block(with_force, pairs, chain, force_weight, rows, spots, radial, wide, edges, weighted, running, pushed, parted):
+    half = iota((TILE, LANES), 1) // TILE
+    within = iota((TILE, LANES), 1) % TILE
+    eye = (within == iota((TILE, LANES), 0)).astype(jnp.float32)
+    upper = half.astype(jnp.float32)
+
+    def one_pair(pair, slot):
+        target = pairs[0, pair]
+        source = pairs[1, pair]
+        before = chain[0, pair]
+        same = jnp.where(target == source, 1.0, 0.0).astype(jnp.float32)
+        spot = spots[source]
+        gap = [wide[target, axis] - spot[axis : axis + 1, :] for axis in range(3)]
+        square = gap[0] * gap[0] + gap[1] * gap[1] + gap[2] * gap[2] + SOFTENING
+        inverse = lax.rsqrt(square)
+        distance = square * inverse
+        ramp = 1.0 - jnp.minimum(square * (1.0 / (CUTOFF * CUTOFF)), 1.0)
+        envelope = ramp * ramp * (1.0 - same * eye)
+        unit = [g * inverse for g in gap]
+        scaled = (distance - (0.5 + STEP * upper)) * (1.0 / BASIS_WIDTH)
+        root_three = math.sqrt(3.0)
+        root_five = math.sqrt(5.0)
+        root_fifteen = math.sqrt(15.0)
+        fifteen = [root_fifteen * u for u in unit]
+        angular = [
+            None,
+            root_three * unit[0],
+            root_three * unit[1],
+            root_three * unit[2],
+            fifteen[0] * unit[1],
+            fifteen[1] * unit[2],
+            (1.5 * root_five) * unit[2] * unit[2] - 0.5 * root_five,
+            fifteen[0] * unit[2],
+            0.5 * (fifteen[0] * unit[0] - fifteen[1] * unit[1]),
+        ]
+        profile = None
+        for q in range(GROUPS):
+            moved = scaled - (2.0 * q * STEP / BASIS_WIDTH)
+            basis = jnp.exp(-(moved * moved)) * envelope
+            if with_force:
+                weight = jnp.where(half == 0, force_weight[2 * q], force_weight[2 * q + 1])
+                profile = weight * basis if profile is None else profile + weight * basis
+            columns = slice(q * LANES, (q + 1) * LANES)
+            edges[slot, 0:TILE, columns] = basis.astype(jnp.bfloat16)
+            for m in range(1, 9):
+                edges[slot, m * TILE : (m + 1) * TILE, columns] = (angular[m] * basis).astype(jnp.bfloat16)
+        near = rows[source]
+        full = near.astype(jnp.float32)
+        for k in range(3 * NB):
+            weighted[slot, k // NB, (k % NB) * TILE : (k % NB + 1) * TILE, :] = (
+                full * radial[k : k + 1, :]
+            ).astype(jnp.bfloat16)
+        for order, (low, high) in enumerate(((0, 1), (1, 4), (4, 9))):
+            lines = slice(low * TILE, high * TILE)
+            message = multiply(edges[slot, lines, :], weighted[slot, order])
+            running[pair + 1, lines, :] = message + running[before, lines, :]
+        if with_force:
+            twice = jnp.concatenate([near, near], axis=0)
+            strength = profile * across(rows[target], twice)
+            line = iota((8, LANES), 0)
+            sums = jnp.zeros((8, LANES), jnp.float32)
+            for axis in range(3):
+                push = strength * unit[axis]
+                pushed[pair + 1, axis] = push + pushed[before, axis]
+                summed = jnp.sum(push, axis=0, keepdims=True)
+                sums = jnp.where(line == axis, summed, sums)
+            parted[pair] = sums
+
+    def two_pairs(step, carried):
+        one_pair(2 * step, 0)
+        one_pair(2 * step + 1, 1)
+        return carried
+
+    count = pairs.shape[1]
+    lax.fori_loop(0, count // 2, two_pairs, 0)
+    for left in range(count // 2 * 2, count):
+        one_pair(left, 0)
+
+
+def renewed(totals, hidden, mix, out_weight):
+    channels = hidden.shape[1]
+
+    def part(m):
+        return totals[m * TILE : (m + 1) * TILE, :] * MESSAGE_SCALE
+
+    vector = part(1) ** 2 + part(2) ** 2 + part(3) ** 2
+    tensor = part(4) ** 2 + part(5) ** 2 + part(6) ** 2 + part(7) ** 2 + part(8) ** 2
+    mixed = mix[0:1, :] * part(0) + mix[1:2, :] * vector + mix[2:3, :] * tensor
+    active = (mixed / (1.0 + jnp.exp(-mixed))).astype(jnp.bfloat16)
+    return (hidden.astype(jnp.float32) + multiply(active, out_weight)).astype(jnp.bfloat16)
+
+
+def step_kernel(
+    edge,
+    counts,
+    pairs,
+    force_weight,
+    sources,
+    wanted,
+    coords,
+    radial,
+    mix,
+    features_far,
+    lift_far,
+    out_weight_far,
+    updated,
+    forces,
+    flag_out,
+    block,
+    lists,
+    table,
+    rows_sent,
+    spots_sent,
+    rows_came,
+    spots_came,
+    gathered,
+    placed,
+    select,
+    hidden,
+    own_rows,
+    own_spots,
+    asked_first,
+    asked_last,
+    asked_spots,
+    near_spots,
+    rows_first,
+    rows_last,
+    spots,
+    wide,
+    edges,
+    weighted,
+    running,
+    pushed,
+    parted,
+    force_sent,
+    force_came,
+    own_force,
+    lift,
+    out_weight,
+    fresh,
+    wants,
+    chain,
+    local,
+    send_list,
+    take_list,
+    send_moved,
+    take_moved,
+    send_spots,
+    take_spots,
+    send_first,
+    take_first,
+    send_near,
+    take_near,
+    send_last,
+    take_last,
+    send_force,
+    take_force,
+):
+    channels = features_far.shape[1]
+    slots = sources.shape[1]
+    tiles = slots // TILE
+    taken = NEAR * CAP
+    own_base = gathered.shape[0] - slots
+    neighbours = [beside(n) for n in range(NEAR)]
+    barrier = pltpu.get_barrier_semaphore()
+    for n in range(NEAR):
+        pl.semaphore_signal(barrier, inc=1, device_id=neighbours[n], device_id_type=MESH)
+    bring = [
+        pltpu.make_async_copy(features_far, gathered.at[pl.ds(own_base, slots), :], local.at[0]),
+        pltpu.make_async_copy(lift_far, lift, local.at[1]),
+        pltpu.make_async_copy(out_weight_far, out_weight, local.at[2]),
+    ]
+    for copy in bring:
+        copy.start()
+
+    row_all = sources[...]
+    code_row = lax.shift_right_logical(row_all, 9)
+    code_row_f = code_row.astype(jnp.float32)
+    level32 = iota((32, slots), 0)
+    tally = jnp.sum(jnp.where(code_row == level32, 1.0, 0.0), axis=1, keepdims=True)
+    tally = jnp.where(iota((32, 1), 0) == 13, 0.0, tally)
+    flag = jnp.broadcast_to(
+        jnp.max(jnp.where(tally > CAP, 1.0, 0.0), axis=0, keepdims=True), (1, LANES)
+    )
+    block[0:1, :] = row_all
+    block[1:2, :] = jnp.zeros((1, slots), jnp.int32)
+    for layer in range(LAYERS):
+        block[1:2, 32 * layer : 32 * layer + 27] = wanted[layer : layer + 1, :]
+    block[1:2, LANES : 2 * LANES] = flag.astype(jnp.int32)
+    pl.semaphore_wait(barrier, NEAR)
+    copies = started(neighbours, lambda n: block, lambda n: lists.at[n], send_list, take_list)
+
+    newest = [jnp.int32(0)] * tiles
+    for pair in range(pairs.shape[1]):
+        target = pairs[0, pair]
+        last = jnp.int32(0)
+        for t in range(tiles):
+            last = jnp.where(target == t, newest[t], last)
+            newest[t] = jnp.where(target == t, pair + 1, newest[t])
+        chain[0, pair] = last
+    for t in range(tiles):
+        chain[1, t] = newest[t]
+    running[0] = jnp.zeros(running.shape[1:], jnp.float32)
+    pushed[0] = jnp.zeros(pushed.shape[1:], jnp.float32)
+    for ref in (rows_first, rows_last):
+        ref[tiles + 13] = jnp.zeros(ref.shape[1:], ref.dtype)
+    spots[:, tiles + 13] = jnp.zeros((2, 8, LANES), jnp.float32)
+    level = iota((LANES, LANES), 0)
+    lane = iota((LANES, LANES), 1)
+    for first in range(slots // LANES):
+        row = row_all[:, first * LANES : (first + 1) * LANES].astype(jnp.float32)
+        turned = jnp.transpose(jnp.broadcast_to(row, (LANES, LANES))).astype(jnp.int32)
+        code = lax.shift_right_logical(turned, 9)
+        slot = jnp.bitwise_and(turned, 511)
+        code_f = code.astype(jnp.float32)
+        total = jnp.zeros((LANES, LANES), jnp.float32)
+        for second in range(first + 1):
+            same = code_f == code_row_f[:, second * LANES : (second + 1) * LANES]
+            if second == first:
+                same = jnp.logical_and(same, lane < level)
+            total = total + jnp.where(same, 1.0, 0.0)
+        rank = jnp.sum(total, axis=1, keepdims=True).astype(jnp.int32)
+        neighbour = code - jnp.where(code >= 13, 1, 0)
+        index = jnp.where(code == 13, own_base + slot, neighbour * CAP + rank)
+        for part in range(gathered.shape[0] // LANES):
+            hit = index == lane + part * LANES
+            select[first * LANES : (first + 1) * LANES, part * LANES : (part + 1) * LANES] = (
+                jnp.where(hit, 1.0, 0.0).astype(jnp.bfloat16)
+            )
+    start = picked_start(coords, counts[0])
+    parts = three_parts(start)
+    placed[:, 0:own_base] = jnp.zeros((8, own_base), jnp.float32)
+    placed[:, own_base:] = start
+    gathered[taken:own_base, :] = jnp.zeros((own_base - taken, channels), jnp.bfloat16)
+    earlier = (iota((slots, slots), 0) < iota((slots, slots), 1)).astype(jnp.float32).astype(jnp.bfloat16)
+    table[...] = jnp.zeros_like(table)
+    spots_sent[...] = jnp.zeros_like(spots_sent)
+    for copy in bring:
+        copy.wait()
+    finish(copies)
+
+    fetch = pltpu.make_async_copy(lists.at[:, 1, pl.ds(0, LANES)], wants, local.at[3])
+    fetch.start()
+    for n in range(NEAR):
+        table[n : n + 1, :] = lists[n, 0:1, :]
+        flag = jnp.maximum(flag, lists[n, 1:2, LANES : 2 * LANES].astype(jnp.float32))
+    held = table[...]
+    number = iota(held.shape, 0)
+    code = number + jnp.where(number >= 13, 1, 0)
+    mine = jnp.logical_and(lax.shift_right_logical(held, 9) == 26 - code, number < NEAR)
+    slot = jnp.bitwise_and(held, 511).astype(jnp.float32)
+    chosen = jnp.where(mine, 1.0, 0.0)
+    rank = jnp.dot(chosen.astype(jnp.bfloat16), earlier, preferred_element_type=jnp.float32)
+    rank = jnp.where(mine, rank, -1.0)
+    order = iota((CAP, slots), 0).astype(jnp.float32)
+    across_lane = iota((CAP, slots), 1).astype(jnp.float32)
+    own_features = gathered[own_base:, :]
+    for n in range(NEAR):
+        hit = rank[n : n + 1, :] == order
+        place = jnp.sum(jnp.where(hit, slot[n : n + 1, :], 0.0), axis=1, keepdims=True)
+        pick = (place == across_lane).astype(jnp.float32).astype(jnp.bfloat16)
+        rows_sent[n] = jnp.dot(pick, own_features, preferred_element_type=jnp.float32).astype(jnp.bfloat16)
+        spots_sent[n, :, 0:CAP] = joined(across(parts, pick))
+        spots_sent[n, 7:8, :] = flag
+    copies = started(
+        neighbours,
+        lambda n: rows_sent.at[n],
+        lambda n: rows_came.at[n],
+        send_moved,
+        take_moved,
+    ) + started(neighbours, lambda n: spots_sent.at[n], lambda n: spots_came.at[n], send_spots, take_spots)
+    fetch.wait()
+    finish(copies)
+
+    gathered[0:taken, :] = rows_came[...].reshape(taken, channels)
+    for n in range(NEAR):
+        placed[:, n * CAP : (n + 1) * CAP] = spots_came[n, :, 0:CAP]
+        flag = jnp.maximum(flag, spots_came[n, 7:8, :])
+    moved = jnp.dot(select[...], gathered[...], preferred_element_type=jnp.float32).astype(jnp.bfloat16)
+    hidden[...] = moved.reshape(hidden.shape)
+    projected = jnp.dot(moved, lift[0], preferred_element_type=jnp.float32).astype(jnp.bfloat16)
+    own_rows[...] = projected.reshape(own_rows.shape)
+    position = joined(across(three_parts(placed[...]), select[...]))
+    high = jnp.where(code_row >= 9, 1, 0) + jnp.where(code_row >= 18, 1, 0)
+    rest = code_row - 9 * high
+    middle = jnp.where(rest >= 3, 1, 0) + jnp.where(rest >= 6, 1, 0)
+    low = rest - 3 * middle
+    line = iota((8, slots), 0)
+    shift = jnp.where(line == 0, high - 1, jnp.where(line == 1, middle - 1, low - 1))
+    position = position + shift.astype(jnp.float32) * edge
+    left_half = iota((8, LANES), 1) < TILE
+    for t in range(tiles):
+        part = position[:, t // 2 * LANES : (t // 2 + 1) * LANES]
+        swapped = pltpu.roll(part, TILE, 1)
+        own_spots[t] = jnp.where(left_half, part, swapped) if t % 2 == 0 else jnp.where(left_half, swapped, part)
+    line8 = iota((8, LANES), 0)
+    for n in range(NEAR):
+        reader = 26 - code_of(n)
+        asked_first[n] = own_rows[wants[n, reader]]
+        near = own_spots[wants[n, reader]]
+        later = pltpu.roll(own_spots[wants[n, 32 + reader]], 3, 0)
+        asked_spots[n] = jnp.where(line8 < 3, near, jnp.where(line8 < 6, later, flag))
+    copies = started(
+        neighbours,
+        lambda n: asked_first.at[n],
+        lambda n: rows_first.at[tiles + code_of(n)],
+        send_first,
+        take_first,
+    ) + started(neighbours, lambda n: asked_spots.at[n], lambda n: near_spots.at[n], send_near, take_near)
+    rows_first[0:tiles] = own_rows[...]
+    for t in range(tiles):
+        own = own_spots[t]
+        spots[0, t] = own
+        spots[1, t] = own
+        turned = jnp.transpose(jnp.broadcast_to(own[None], (16, 8, LANES)).reshape(LANES, LANES))
+        for axis in range(3):
+            wide[t, axis] = jnp.broadcast_to(turned[:TILE, axis : axis + 1], (TILE, LANES))
+    finish(copies)
+    for n in range(NEAR):
+        code = code_of(n)
+        came = near_spots[n]
+        flag = jnp.maximum(flag, came[7:8, :])
+        for axis, step in enumerate(steps_of(code)):
+            for layer in range(2):
+                where = axis + 3 * layer
+                spots[layer, tiles + code, axis : axis + 1, :] = came[where : where + 1, :] + step * edge
+
+    pair_block(
+        False, pairs, chain, force_weight, rows_first, spots.at[0], radial.at[0], wide, edges, weighted, running, None, None
+    )
+    for t in range(tiles):
+        new = renewed(running[chain[1, t]], hidden[t], mix[0], out_weight[0])
+        hidden[t] = new
+        later = multiply(new, lift[1]).astype(jnp.bfloat16)
+        rows_last[t] = later
+        own_rows[t] = later
+    for n in range(NEAR):
+        asked_last[n] = own_rows[wants[n, 32 + 26 - code_of(n)]]
+    copies = started(
+        neighbours,
+        lambda n: asked_last.at[n],
+        lambda n: rows_last.at[tiles + code_of(n)],
+        send_last,
+        take_last,
+    )
+    finish(copies)
+
+    pair_block(
+        True, pairs, chain, force_weight, rows_last, spots.at[1], radial.at[1], wide, edges, weighted, running, pushed, parted
+    )
+    factor = 0.5 / math.sqrt(channels)
+
+    def add_part(pair, carried):
+        source = pairs[1, pair]
+        part = parted[pair]
+        return tuple(
+            held + jnp.where(source == b, part, jnp.zeros_like(part)) for b, held in enumerate(carried)
+        )
+
+    sums = lax.fori_loop(
+        0,
+        pairs.shape[1],
+        add_part,
+        tuple(jnp.zeros((8, LANES), jnp.float32) for _ in range(tiles + 27)),
+    )
+    sums = [(held + pltpu.roll(held, TILE, 1)) * factor for held in sums]
+    for n in range(NEAR):
+        force_sent[n] = jnp.where(line8 < 7, -sums[tiles + code_of(n)], flag)
+    copies = started(
+        neighbours, lambda n: force_sent.at[n], lambda n: force_came.at[n], send_force, take_force
+    )
+    lane64 = iota((TILE, LANES), 1)
+    for t in range(tiles):
+        fresh[t * TILE : (t + 1) * TILE, :] = renewed(running[chain[1, t]], hidden[t], mix[1], out_weight[1])
+        push = pushed[chain[1, t]]
+        columns = jnp.zeros((TILE, LANES), jnp.float32)
+        for axis in range(3):
+            columns = jnp.where(lane64 == axis, jnp.sum(push[axis], axis=1, keepdims=True), columns)
+        turned = jnp.transpose(jnp.concatenate([columns, columns], axis=0))[0:8, :]
+        own_force[t] = turned * factor - sums[t]
+    away = pltpu.make_async_copy(fresh, updated, local.at[0])
+    away.start()
+    finish(copies)
+    totals = [own_force[t] for t in range(tiles)]
+    for n in range(NEAR):
+        tile = wants[n, 32 + 26 - code_of(n)]
+        came = force_came[n]
+        flag = jnp.maximum(flag, came[7:8, :])
+        totals = [held + jnp.where(tile == t, came, jnp.zeros_like(came)) for t, held in enumerate(totals)]
+    for part in range(tiles // 2):
+        both = jnp.where(left_half, totals[2 * part], totals[2 * part + 1])
+        forces[:, part * LANES : (part + 1) * LANES] = both[0:3, :]
+    flag_out[...] = flag.astype(jnp.int32)
+    away.wait()
+
+
+def body(
+    features,
+    coords,
+    counts,
+    sources,
+    wanted,
+    pairs,
+    lifting_weight,
+    radial_weight,
+    mix_weight,
+    out_weight,
+    force_weight,
+):
+    slots, channels = features.shape[3], features.shape[4]
+    tiles = slots // TILE
+    edge = float((slots / DENSITY) ** (1.0 / 3.0))
+    count = pairs.shape[4]
+    held = -(-NEAR * CAP // LANES) * LANES + slots
+    shape = jax.ShapeDtypeStruct
+    far, bits = jnp.float32, jnp.bfloat16
+
+    def kernel(*refs):
+        step_kernel(edge, *refs)
+
+    updated, forces, flag = pl.pallas_call(
+        kernel,
+        name="whole_step",
+        out_shape=[
+            shape((slots, channels), bits),
+            shape((3, slots), far),
+            shape((1, LANES), jnp.int32),
+        ],
+        in_specs=[SMEM] * 3 + [VMEM] * 5 + [ANY] * 3,
+        out_specs=[ANY, VMEM, VMEM],
+        scratch_shapes=[
+            pltpu.VMEM((2, slots), jnp.int32),
+            pltpu.VMEM((NEAR, 2, slots), jnp.int32),
+            pltpu.VMEM((32, slots), jnp.int32),
+            pltpu.VMEM((NEAR, CAP, channels), bits),
+            pltpu.VMEM((NEAR, 8, LANES), far),
+            pltpu.VMEM((NEAR, CAP, channels), bits),
+            pltpu.VMEM((NEAR, 8, LANES), far),
+            pltpu.VMEM((held, channels), bits),
+            pltpu.VMEM((8, held), far),
+            pltpu.VMEM((slots, held), bits),
+            pltpu.VMEM((tiles, TILE, channels), bits),
+            pltpu.VMEM((tiles, TILE, channels), bits),
+            pltpu.VMEM((tiles, 8, LANES), far),
+            pltpu.VMEM((NEAR, TILE, channels), bits),
+            pltpu.VMEM((NEAR, TILE, channels), bits),
+            pltpu.VMEM((NEAR, 8, LANES), far),
+            pltpu.VMEM((NEAR, 8, LANES), far),
+            pltpu.VMEM((tiles + 27, TILE, channels), bits),
+            pltpu.VMEM((tiles + 27, TILE, channels), bits),
+            pltpu.VMEM((2, tiles + 27, 8, LANES), far),
+            pltpu.VMEM((tiles, 3, TILE, LANES), far),
+            pltpu.VMEM((2, 9 * TILE, NB * TILE), bits),
+            pltpu.VMEM((2, 3, NB * TILE, channels), bits),
+            pltpu.VMEM((count + 1, 9 * TILE, channels), far),
+            pltpu.VMEM((count + 1, 3, TILE, LANES), far),
+            pltpu.VMEM((count, 8, LANES), far),
+            pltpu.VMEM((NEAR, 8, LANES), far),
+            pltpu.VMEM((NEAR, 8, LANES), far),
+            pltpu.VMEM((tiles, 8, LANES), far),
+            pltpu.VMEM((LAYERS, channels, channels), bits),
+            pltpu.VMEM((LAYERS, channels, channels), bits),
+            pltpu.VMEM((slots, channels), bits),
+            pltpu.SMEM((NEAR, LANES), jnp.int32),
+            pltpu.SMEM((2, LANES), jnp.int32),
+            pltpu.SemaphoreType.DMA((4,)),
+        ]
+        + [pltpu.SemaphoreType.DMA((NEAR,))] * 14,
+        compiler_params=pltpu.CompilerParams(
+            collective_id=1, has_side_effects=True, vmem_limit_bytes=56 * 1024 * 1024
+        ),
+    )(
+        counts.reshape(1),
+        pairs.reshape(2, count),
+        force_weight,
+        sources.reshape(1, slots),
+        wanted.reshape(LAYERS, 27),
+        coords.reshape(3, slots),
+        radial_weight.reshape(LAYERS, 3 * NB, channels),
+        mix_weight,
+        features.reshape(slots, channels),
+        lifting_weight,
+        out_weight,
+    )
+    updated = updated.reshape(features.shape)
+    forces = forces.reshape(coords.shape)
+    return lax.cond(
+        flag[0, 0] > 0,
+        lambda: whole_path(
+            features,
+            coords,
+            counts,
+            sources,
+            wanted,
+            pairs,
+            lifting_weight,
+            radial_weight,
+            mix_weight,
+            out_weight,
+            force_weight,
+        ),
+        lambda: (updated, forces),
+    )
+
+
 def solution(mesh):
     placed = (
         P("gx", "gy", "gz", None, None),

time: 586 us -> 86.4 us (0.15); the launches traced: 578 us -> 86.2 us
  other arithmetic: 233 us -> 0 us
  local copies, waits for them, and re-layouts: 154 us -> 4.74 us
  starting transfers between devices: 130 us -> 0 us
  Pallas kernels: 0 us -> 79.5 us
  matrix products: 29 us -> 0 us
  waiting for transfers between devices: 20.2 us -> 0 us
  loops' own time: 8.78 us -> 0.01 us
    scatter-add x64 -> x0, other arithmetic: 142 us -> none  [the longest x32 83.2 us: one_block(): totals = totals.at[targets].add(message)]
    ppermute x42 -> x0, starting transfers between devices: 130 us -> none  [the longest x21 70.5 us: padded(): lax.ppermute(head, axis, [((i + 1) % count, i) for i in range(count)])]
    pallas_call x0 -> x1, Pallas kernels: none -> 79.5 us  [body(): pl.pallas_call(kernel, name='whole_step', out_shape=[shape((slots, channe...]
    gather x183 -> x0, local copies, waits for them, and re-layouts: 72.8 us -> none  [the longest x64 18.4 us: one_block(): source_places[targets]]
    slice x188 -> x0, local copies, waits for them, and re-layouts: 34.3 us -> none  [the longest x32 24.2 us: one_block(): pair_list[1]]
    dot_general x117 -> x0, matrix products: 29 us -> none  [the longest x116 28.8 us: multiply(): return jnp.dot(left, right, preferred_element_type=jnp.float32)]
    convert_element_type x130 -> x0, other arithmetic: 20.9 us -> none  [the longest x32 11.9 us: pair_terms(): edges = (angular * basis[None]).astype(jnp.bfloat16)]
    ppermute x42 -> x0, waiting for transfers between devices: 20.2 us -> none  [the longest x21 16.1 us: padded(): lax.ppermute(head, axis, [((i + 1) % count, i) for i in range(count)])]
  transfers between devices with their start and end apart: 42 -> 0, of which waited for: 16 -> 0; matrix products, arithmetic and copies ran while one was open for 7% -> 0% of each run, Pallas kernels for 0% -> 0%
where the time goes in v2:
time: 86.4 us; the launch traced here: 86.2 us
  Pallas kernels  79.5 us (92%)
  local copies, waits for them, and re-layouts  4.74 us (5%)
  between operations  1.86 us (2%)
    pallas_call x1, Pallas kernels, body(): pl.pallas_call(kernel, name='whole_step', out_shape=[shape((slots, channe...  79.5 us
    unnamed x3, local copies, waits for them, and re-layouts  4.14 us

profile of v2, /device:TPU:1, one launch (start us, length us, event | category | flops | bytes accessed | tf_op | source)
XLA Modules:
  0.0 86.2 jit_solution(2994275942830498558)
XLA Ops:
  0.6 1.3 %copy.195 = f32[1,1,1,3,512]{4,3,2,1,0:T(4,128)} copy(f32[1,1,1,3,512]{4,2,3,1,0:T(1,128)} %param.23) | data formatting | bytes 12288
  1.9 1.3 %copy.184.refs_7_ = f32[2,3,128]{2,1,0:T(4,128)} copy(f32[2,3,128]{2,0,1:T(2,128)} %param.30) | data formatting | bytes 6144 | tf_op args[8]
  3.9 79.5 %whole_step.1 = (bf16[512,128]{1,0:T(8,128)(2,1)}, f32[3,512]{1,0:T(4,128)S(1)}, s32[1,128]{1,0:T(1,128)}) custom-call(s32[1]{0:T(128)} %bitcast.317.refs_0_, s32[2,32]{1,0:T(2,128)} %bitcast.354, f32[8]{0:T(128)} %refs_2_.1, s32[1,512]{1,0:T(1,128)} %bitcast.357, s32[2,27]{1,0:T(2,128)} %bitcast.360, f32[3,512]{1,0:T(4,128)} %bitcast.359, ...), custom_call_target="tpu_custom_call" | custom-call | tf_op jit(solution)/shard_map/whole_step/pallas_call | solution.py:752
  84.0 0.6 conditional.1
  84.0 0.6 copy.188
  84.6 1.6 %copy.259 = bf16[1,1,1,512,128]{4,3,2,1,0:T(8,128)(2,1)} copy(bf16[1,1,1,512,128]{4,3,2,1,0:T(8,128)(2,1)} %bitcast.109) | data formatting | bytes 262144

commit v3 on v2

--- a/solution.py
+++ b/solution.py
@@ -266,6 +266,11 @@
 ANY = pl.BlockSpec(memory_space=pl.ANY)
 
 
+CHUNK = 16
+SHAPED = 1
+SUMMED = 4
+
+
 def code_of(n):
     return n + (1 if n >= 13 else 0)
 
@@ -282,20 +287,24 @@
     return tuple(found)
 
 
-def started(neighbours, source_of, target_of, send, receive):
-    copies = []
-    for n in range(NEAR):
-        copy = pltpu.make_async_remote_copy(
-            src_ref=source_of(n),
-            dst_ref=target_of(NEAR - 1 - n),
-            send_sem=send.at[n],
-            recv_sem=receive.at[NEAR - 1 - n],
+FAR_FIRST = sorted(range(NEAR), key=lambda n: -sum(abs(step) for step in steps_of(code_of(n))))
+
+
+def started(neighbours, source_of, landing, first, send, receive):
+    def copy_of(source, target, n):
+        return pltpu.make_async_remote_copy(
+            src_ref=source,
+            dst_ref=target,
+            send_sem=send,
+            recv_sem=receive,
             device_id=neighbours[n],
             device_id_type=MESH,
         )
-        copy.start()
-        copies.append(copy)
-    return copies
+
+    for n in FAR_FIRST:
+        copy_of(source_of(n), landing.at[first + NEAR - 1 - n], n).start()
+    whole = landing.at[pl.ds(first, NEAR)]
+    return [copy_of(whole, whole, 0)]
 
 
 def finish(copies):
@@ -323,59 +332,91 @@
 
 
 def picked_start(coords, count):
-    slots = coords.shape[1]
-    slot = iota((3, slots), 1)
-    start = jnp.where(slot < count, coords[...], FAR_AWAY + DEAD_SPACING * slot.astype(jnp.float32))
-    return jnp.concatenate([start, jnp.zeros((5, slots), jnp.float32)], axis=0)
-
-
-def pair_block(with_force, pairs, chain, force_weight, rows, spots, radial, wide, edges, weighted, running, pushed, parted):
-    half = iota((TILE, LANES), 1) // TILE
-    within = iota((TILE, LANES), 1) % TILE
-    eye = (within == iota((TILE, LANES), 0)).astype(jnp.float32)
+    slots = coords.shape[1] // 3
+    rows = [coords[:, axis * slots : (axis + 1) * slots] for axis in range(3)]
+    rows = jnp.concatenate(rows + [jnp.zeros((5, slots), jnp.float32)], axis=0)
+    slot = iota((8, slots), 1)
+    start = jnp.where(slot < count, rows, FAR_AWAY + DEAD_SPACING * slot.astype(jnp.float32))
+    return jnp.where(iota((8, slots), 0) < 3, start, 0.0)
+
+
+def row_of(source):
+    return source - jnp.where(source > 21, 1, 0)
+
+
+def over_pairs(count, together, one_pair):
+    def some(step, carried):
+        for slot in range(together):
+            one_pair(step * together + slot, slot)
+        return carried
+
+    lax.fori_loop(0, count // together, some, 0)
+    for left in range(count // together * together, count):
+        one_pair(left, 0)
+
+
+def shape_pairs(with_force, pairs, force_weight, spots, wide, edges, pull):
+    half = iota((CHUNK, LANES), 1) // TILE
+    within = iota((CHUNK, LANES), 1) % TILE
+    level = iota((CHUNK, LANES), 0)
     upper = half.astype(jnp.float32)
+    root_three = math.sqrt(3.0)
+    root_five = math.sqrt(5.0)
+    root_fifteen = math.sqrt(15.0)
+    if with_force:
+        weights = [jnp.where(half == 0, force_weight[2 * q], force_weight[2 * q + 1]) for q in range(GROUPS)]
 
     def one_pair(pair, slot):
         target = pairs[0, pair]
         source = pairs[1, pair]
+        drop = jnp.where(target == source, 1.0, 0.0).astype(jnp.float32)
+        spot = spots[row_of(source)]
+        for top in range(0, TILE, CHUNK):
+            lines = slice(top, top + CHUNK)
+            gap = [wide[target, axis, lines, :] - spot[axis : axis + 1, :] for axis in range(3)]
+            square = gap[0] * gap[0] + gap[1] * gap[1] + gap[2] * gap[2] + SOFTENING
+            inverse = lax.rsqrt(square)
+            ramp = 1.0 - jnp.minimum(square * (1.0 / (CUTOFF * CUTOFF)), 1.0)
+            eye = jnp.where(within == level + top, drop, 0.0)
+            envelope = ramp * ramp * (1.0 - eye)
+            unit = [g * inverse for g in gap]
+            scaled = (square * inverse) * (1.0 / BASIS_WIDTH) - (0.5 + STEP * upper) * (1.0 / BASIS_WIDTH)
+            fifteen = [root_fifteen * u for u in unit]
+            angular = [
+                None,
+                root_three * unit[0],
+                root_three * unit[1],
+                root_three * unit[2],
+                fifteen[0] * unit[1],
+                fifteen[1] * unit[2],
+                (1.5 * root_five) * unit[2] * unit[2] - 0.5 * root_five,
+                fifteen[0] * unit[2],
+                0.5 * (fifteen[0] * unit[0] - fifteen[1] * unit[1]),
+            ]
+            profile = None
+            for q in range(GROUPS):
+                moved = scaled - (2.0 * q * STEP / BASIS_WIDTH)
+                basis = jnp.exp(-(moved * moved)) * envelope
+                if with_force:
+                    part = weights[q] * basis
+                    profile = part if profile is None else profile + part
+                columns = slice(q * LANES, (q + 1) * LANES)
+                edges[pair, lines, columns] = basis.astype(jnp.bfloat16)
+                for m in range(1, 9):
+                    edges[pair, m * TILE + top : m * TILE + top + CHUNK, columns] = (
+                        angular[m] * basis
+                    ).astype(jnp.bfloat16)
+            if with_force:
+                for axis in range(3):
+                    pull[pair, axis, lines, :] = profile * unit[axis]
+
+    over_pairs(pairs.shape[1], SHAPED, one_pair)
+
+
+def sum_pairs(with_force, pairs, chain, rows, radial, edges, weighted, running, pull, pushed, parted):
+    def one_pair(pair, slot):
         before = chain[0, pair]
-        same = jnp.where(target == source, 1.0, 0.0).astype(jnp.float32)
-        spot = spots[source]
-        gap = [wide[target, axis] - spot[axis : axis + 1, :] for axis in range(3)]
-        square = gap[0] * gap[0] + gap[1] * gap[1] + gap[2] * gap[2] + SOFTENING
-        inverse = lax.rsqrt(square)
-        distance = square * inverse
-        ramp = 1.0 - jnp.minimum(square * (1.0 / (CUTOFF * CUTOFF)), 1.0)
-        envelope = ramp * ramp * (1.0 - same * eye)
-        unit = [g * inverse for g in gap]
-        scaled = (distance - (0.5 + STEP * upper)) * (1.0 / BASIS_WIDTH)
-        root_three = math.sqrt(3.0)
-        root_five = math.sqrt(5.0)
-        root_fifteen = math.sqrt(15.0)
-        fifteen = [root_fifteen * u for u in unit]
-        angular = [
-            None,
-            root_three * unit[0],
-            root_three * unit[1],
-            root_three * unit[2],
-            fifteen[0] * unit[1],
-            fifteen[1] * unit[2],
-            (1.5 * root_five) * unit[2] * unit[2] - 0.5 * root_five,
-            fifteen[0] * unit[2],
-            0.5 * (fifteen[0] * unit[0] - fifteen[1] * unit[1]),
-        ]
-        profile = None
-        for q in range(GROUPS):
-            moved = scaled - (2.0 * q * STEP / BASIS_WIDTH)
-            basis = jnp.exp(-(moved * moved)) * envelope
-            if with_force:
-                weight = jnp.where(half == 0, force_weight[2 * q], force_weight[2 * q + 1])
-                profile = weight * basis if profile is None else profile + weight * basis
-            columns = slice(q * LANES, (q + 1) * LANES)
-            edges[slot, 0:TILE, columns] = basis.astype(jnp.bfloat16)
-            for m in range(1, 9):
-                edges[slot, m * TILE : (m + 1) * TILE, columns] = (angular[m] * basis).astype(jnp.bfloat16)
-        near = rows[source]
+        near = rows[row_of(pairs[1, pair])]
         full = near.astype(jnp.float32)
         for k in range(3 * NB):
             weighted[slot, k // NB, (k % NB) * TILE : (k % NB + 1) * TILE, :] = (
@@ -383,29 +424,20 @@
             ).astype(jnp.bfloat16)
         for order, (low, high) in enumerate(((0, 1), (1, 4), (4, 9))):
             lines = slice(low * TILE, high * TILE)
-            message = multiply(edges[slot, lines, :], weighted[slot, order])
+            message = multiply(edges[pair, lines, :], weighted[slot, order])
             running[pair + 1, lines, :] = message + running[before, lines, :]
         if with_force:
-            twice = jnp.concatenate([near, near], axis=0)
-            strength = profile * across(rows[target], twice)
+            inner = across(rows[pairs[0, pair]], jnp.concatenate([near, near], axis=0))
             line = iota((8, LANES), 0)
             sums = jnp.zeros((8, LANES), jnp.float32)
             for axis in range(3):
-                push = strength * unit[axis]
+                push = pull[pair, axis] * inner
                 pushed[pair + 1, axis] = push + pushed[before, axis]
                 summed = jnp.sum(push, axis=0, keepdims=True)
                 sums = jnp.where(line == axis, summed, sums)
             parted[pair] = sums
 
-    def two_pairs(step, carried):
-        one_pair(2 * step, 0)
-        one_pair(2 * step + 1, 1)
-        return carried
-
-    count = pairs.shape[1]
-    lax.fori_loop(0, count // 2, two_pairs, 0)
-    for left in range(count // 2 * 2, count):
-        one_pair(left, 0)
+    over_pairs(pairs.shape[1], SUMMED, one_pair)
 
 
 def renewed(totals, hidden, mix, out_weight):
@@ -440,6 +472,7 @@
     block,
     lists,
     table,
+    picks,
     rows_sent,
     spots_sent,
     rows_came,
@@ -459,6 +492,7 @@
     spots,
     wide,
     edges,
+    pull,
     weighted,
     running,
     pushed,
@@ -468,7 +502,6 @@
     own_force,
     lift,
     out_weight,
-    fresh,
     wants,
     chain,
     local,
@@ -519,7 +552,7 @@
         block[1:2, 32 * layer : 32 * layer + 27] = wanted[layer : layer + 1, :]
     block[1:2, LANES : 2 * LANES] = flag.astype(jnp.int32)
     pl.semaphore_wait(barrier, NEAR)
-    copies = started(neighbours, lambda n: block, lambda n: lists.at[n], send_list, take_list)
+    copies = started(neighbours, lambda n: block, lists, 0, send_list, take_list)
 
     newest = [jnp.int32(0)] * tiles
     for pair in range(pairs.shape[1]):
@@ -533,9 +566,6 @@
         chain[1, t] = newest[t]
     running[0] = jnp.zeros(running.shape[1:], jnp.float32)
     pushed[0] = jnp.zeros(pushed.shape[1:], jnp.float32)
-    for ref in (rows_first, rows_last):
-        ref[tiles + 13] = jnp.zeros(ref.shape[1:], ref.dtype)
-    spots[:, tiles + 13] = jnp.zeros((2, 8, LANES), jnp.float32)
     level = iota((LANES, LANES), 0)
     lane = iota((LANES, LANES), 1)
     for first in range(slots // LANES):
@@ -589,17 +619,15 @@
     for n in range(NEAR):
         hit = rank[n : n + 1, :] == order
         place = jnp.sum(jnp.where(hit, slot[n : n + 1, :], 0.0), axis=1, keepdims=True)
-        pick = (place == across_lane).astype(jnp.float32).astype(jnp.bfloat16)
-        rows_sent[n] = jnp.dot(pick, own_features, preferred_element_type=jnp.float32).astype(jnp.bfloat16)
-        spots_sent[n, :, 0:CAP] = joined(across(parts, pick))
+        picks[n * CAP : (n + 1) * CAP, :] = jnp.where(place == across_lane, 1.0, 0.0).astype(jnp.bfloat16)
+    sent = jnp.dot(picks[...], own_features, preferred_element_type=jnp.float32).astype(jnp.bfloat16)
+    rows_sent[...] = sent.reshape(rows_sent.shape)
+    sent = joined(across(parts, picks[...]))
+    for n in range(NEAR):
+        spots_sent[n, :, 0:CAP] = sent[:, n * CAP : (n + 1) * CAP]
         spots_sent[n, 7:8, :] = flag
-    copies = started(
-        neighbours,
-        lambda n: rows_sent.at[n],
-        lambda n: rows_came.at[n],
-        send_moved,
-        take_moved,
-    ) + started(neighbours, lambda n: spots_sent.at[n], lambda n: spots_came.at[n], send_spots, take_spots)
+    copies = started(neighbours, lambda n: rows_sent.at[n], rows_came, 0, send_moved, take_moved)
+    copies += started(neighbours, lambda n: spots_sent.at[n], spots_came, 0, send_spots, take_spots)
     fetch.wait()
     finish(copies)
 
@@ -631,13 +659,8 @@
         near = own_spots[wants[n, reader]]
         later = pltpu.roll(own_spots[wants[n, 32 + reader]], 3, 0)
         asked_spots[n] = jnp.where(line8 < 3, near, jnp.where(line8 < 6, later, flag))
-    copies = started(
-        neighbours,
-        lambda n: asked_first.at[n],
-        lambda n: rows_first.at[tiles + code_of(n)],
-        send_first,
-        take_first,
-    ) + started(neighbours, lambda n: asked_spots.at[n], lambda n: near_spots.at[n], send_near, take_near)
+    placing = started(neighbours, lambda n: asked_spots.at[n], near_spots, 0, send_near, take_near)
+    copies = started(neighbours, lambda n: asked_first.at[n], rows_first, tiles, send_first, take_first)
     rows_first[0:tiles] = own_rows[...]
     for t in range(tiles):
         own = own_spots[t]
@@ -646,39 +669,31 @@
         turned = jnp.transpose(jnp.broadcast_to(own[None], (16, 8, LANES)).reshape(LANES, LANES))
         for axis in range(3):
             wide[t, axis] = jnp.broadcast_to(turned[:TILE, axis : axis + 1], (TILE, LANES))
-    finish(copies)
-    for n in range(NEAR):
-        code = code_of(n)
+    finish(placing)
+    for n in range(NEAR):
         came = near_spots[n]
         flag = jnp.maximum(flag, came[7:8, :])
-        for axis, step in enumerate(steps_of(code)):
+        for axis, step in enumerate(steps_of(code_of(n))):
             for layer in range(2):
                 where = axis + 3 * layer
-                spots[layer, tiles + code, axis : axis + 1, :] = came[where : where + 1, :] + step * edge
-
-    pair_block(
-        False, pairs, chain, force_weight, rows_first, spots.at[0], radial.at[0], wide, edges, weighted, running, None, None
-    )
+                spots[layer, tiles + n, axis : axis + 1, :] = came[where : where + 1, :] + step * edge
+
+    shape_pairs(False, pairs, force_weight, spots.at[0], wide, edges, pull)
+    finish(copies)
+    sum_pairs(False, pairs, chain, rows_first, radial.at[0], edges, weighted, running, pull, pushed, parted)
     for t in range(tiles):
-        new = renewed(running[chain[1, t]], hidden[t], mix[0], out_weight[0])
+        new = renewed(running[chain[1, t]], hidden[t], mix[:, 0], out_weight[0])
         hidden[t] = new
         later = multiply(new, lift[1]).astype(jnp.bfloat16)
         rows_last[t] = later
         own_rows[t] = later
     for n in range(NEAR):
         asked_last[n] = own_rows[wants[n, 32 + 26 - code_of(n)]]
-    copies = started(
-        neighbours,
-        lambda n: asked_last.at[n],
-        lambda n: rows_last.at[tiles + code_of(n)],
-        send_last,
-        take_last,
-    )
+    copies = started(neighbours, lambda n: asked_last.at[n], rows_last, tiles, send_last, take_last)
+    shape_pairs(True, pairs, force_weight, spots.at[1], wide, edges, pull)
     finish(copies)
 
-    pair_block(
-        True, pairs, chain, force_weight, rows_last, spots.at[1], radial.at[1], wide, edges, weighted, running, pushed, parted
-    )
+    sum_pairs(True, pairs, chain, rows_last, radial.at[1], edges, weighted, running, pull, pushed, parted)
     factor = 0.5 / math.sqrt(channels)
 
     def add_part(pair, carried):
@@ -697,20 +712,16 @@
     sums = [(held + pltpu.roll(held, TILE, 1)) * factor for held in sums]
     for n in range(NEAR):
         force_sent[n] = jnp.where(line8 < 7, -sums[tiles + code_of(n)], flag)
-    copies = started(
-        neighbours, lambda n: force_sent.at[n], lambda n: force_came.at[n], send_force, take_force
-    )
+    copies = started(neighbours, lambda n: force_sent.at[n], force_came, 0, send_force, take_force)
     lane64 = iota((TILE, LANES), 1)
     for t in range(tiles):
-        fresh[t * TILE : (t + 1) * TILE, :] = renewed(running[chain[1, t]], hidden[t], mix[1], out_weight[1])
+        updated[t * TILE : (t + 1) * TILE, :] = renewed(running[chain[1, t]], hidden[t], mix[:, 1], out_weight[1])
         push = pushed[chain[1, t]]
         columns = jnp.zeros((TILE, LANES), jnp.float32)
         for axis in range(3):
             columns = jnp.where(lane64 == axis, jnp.sum(push[axis], axis=1, keepdims=True), columns)
         turned = jnp.transpose(jnp.concatenate([columns, columns], axis=0))[0:8, :]
         own_force[t] = turned * factor - sums[t]
-    away = pltpu.make_async_copy(fresh, updated, local.at[0])
-    away.start()
     finish(copies)
     totals = [own_force[t] for t in range(tiles)]
     for n in range(NEAR):
@@ -720,9 +731,10 @@
         totals = [held + jnp.where(tile == t, came, jnp.zeros_like(came)) for t, held in enumerate(totals)]
     for part in range(tiles // 2):
         both = jnp.where(left_half, totals[2 * part], totals[2 * part + 1])
-        forces[:, part * LANES : (part + 1) * LANES] = both[0:3, :]
+        for axis in range(3):
+            column = axis * slots + part * LANES
+            forces[:, column : column + LANES] = both[axis : axis + 1, :]
     flag_out[...] = flag.astype(jnp.int32)
-    away.wait()
 
 
 def body(
@@ -754,15 +766,16 @@
         name="whole_step",
         out_shape=[
             shape((slots, channels), bits),
-            shape((3, slots), far),
+            shape((1, 3 * slots), far),
             shape((1, LANES), jnp.int32),
         ],
         in_specs=[SMEM] * 3 + [VMEM] * 5 + [ANY] * 3,
-        out_specs=[ANY, VMEM, VMEM],
+        out_specs=[VMEM] * 3,
         scratch_shapes=[
             pltpu.VMEM((2, slots), jnp.int32),
             pltpu.VMEM((NEAR, 2, slots), jnp.int32),
             pltpu.VMEM((32, slots), jnp.int32),
+            pltpu.VMEM((NEAR * CAP, slots), bits),
             pltpu.VMEM((NEAR, CAP, channels), bits),
             pltpu.VMEM((NEAR, 8, LANES), far),
             pltpu.VMEM((NEAR, CAP, channels), bits),
@@ -777,12 +790,13 @@
             pltpu.VMEM((NEAR, TILE, channels), bits),
             pltpu.VMEM((NEAR, 8, LANES), far),
             pltpu.VMEM((NEAR, 8, LANES), far),
-            pltpu.VMEM((tiles + 27, TILE, channels), bits),
-            pltpu.VMEM((tiles + 27, TILE, channels), bits),
-            pltpu.VMEM((2, tiles + 27, 8, LANES), far),
+            pltpu.VMEM((tiles + NEAR, TILE, channels), bits),
+            pltpu.VMEM((tiles + NEAR, TILE, channels), bits),
+            pltpu.VMEM((2, tiles + NEAR, 8, LANES), far),
             pltpu.VMEM((tiles, 3, TILE, LANES), far),
-            pltpu.VMEM((2, 9 * TILE, NB * TILE), bits),
-            pltpu.VMEM((2, 3, NB * TILE, channels), bits),
+            pltpu.VMEM((count, 9 * TILE, NB * TILE), bits),
+            pltpu.VMEM((count, 3, TILE, LANES), far),
+            pltpu.VMEM((SUMMED, 3, NB * TILE, channels), bits),
             pltpu.VMEM((count + 1, 9 * TILE, channels), far),
             pltpu.VMEM((count + 1, 3, TILE, LANES), far),
             pltpu.VMEM((count, 8, LANES), far),
@@ -791,12 +805,11 @@
             pltpu.VMEM((tiles, 8, LANES), far),
             pltpu.VMEM((LAYERS, channels, channels), bits),
             pltpu.VMEM((LAYERS, channels, channels), bits),
-            pltpu.VMEM((slots, channels), bits),
             pltpu.SMEM((NEAR, LANES), jnp.int32),
             pltpu.SMEM((2, LANES), jnp.int32),
             pltpu.SemaphoreType.DMA((4,)),
         ]
-        + [pltpu.SemaphoreType.DMA((NEAR,))] * 14,
+        + [pltpu.SemaphoreType.DMA] * 14,
         compiler_params=pltpu.CompilerParams(
             collective_id=1, has_side_effects=True, vmem_limit_bytes=56 * 1024 * 1024
         ),
@@ -806,9 +819,9 @@
         force_weight,
         sources.reshape(1, slots),
         wanted.reshape(LAYERS, 27),
-        coords.reshape(3, slots),
+        coords.reshape(1, 3 * slots),
         radial_weight.reshape(LAYERS, 3 * NB, channels),
-        mix_weight,
+        jnp.transpose(mix_weight, (1, 0, 2)),
         features.reshape(slots, channels),
         lifting_weight,
         out_weight,

time: 86.4 us -> 73.7 us (0.85)
  Pallas kernels: 79.5 us -> 68.4 us
  local copies, waits for them, and re-layouts: 4.74 us -> 2.85 us
    pallas_call x1, Pallas kernels: 79.5 us -> 68.4 us  [body(): pl.pallas_call(kernel, name='whole_step', out_shape=[shape((slots, channe...]
    unnamed x3 -> x2, local copies, waits for them, and re-layouts: 4.14 us -> 2.85 us
where the time goes in v3:
time: 73.7 us; the launch traced here: 73.4 us
  Pallas kernels  68.4 us (93%)
  local copies, waits for them, and re-layouts  2.85 us (4%)
  between operations  1.91 us (3%)
    pallas_call x1, Pallas kernels, body(): pl.pallas_call(kernel, name='whole_step', out_shape=[shape((slots, channe...  68.4 us
    unnamed x2, local copies, waits for them, and re-layouts  2.85 us

profile of v3, /device:TPU:1, one launch (start us, length us, event | category | flops | bytes accessed | tf_op | source)
XLA Modules:
  0.0 73.4 jit_solution(3048285057227982435)
XLA Ops:
  1.3 68.4 %whole_step.1 = (bf16[512,128]{1,0:T(8,128)(2,1)}, f32[1,1536]{1,0:T(1,128)}, s32[1,128]{1,0:T(1,128)}) custom-call(s32[1]{0:T(128)} %bitcast.316.refs_0_, s32[2,32]{1,0:T(2,128)} %bitcast.353, f32[8]{0:T(128)} %refs_2_.1, s32[1,512]{1,0:T(1,128)} %bitcast.356, s32[2,27]{1,0:T(2,128)} %bitcast.358, f32[1,1536]{1,0:T(1,128)} %bitcast.362, ...), custom_call_target="tpu_custom_call" | custom-call | tf_op jit(solution)/shard_map/whole_step/pallas_call | solution.py:764
  70.3 0.2 conditional.1
  70.6 1.6 %copy.252 = bf16[1,1,1,512,128]{4,3,2,1,0:T(8,128)(2,1)} copy(bf16[1,1,1,512,128]{4,3,2,1,0:T(8,128)(2,1)} %bitcast.110) | data formatting | bytes 262144
  72.1 1.3 %copy.253 = f32[1,1,1,3,512]{4,2,3,1,0:T(1,128)} copy(f32[1,1,1,3,512]{4,2,3,1,0:T(1,128)} %get-tuple-element.769) | data formatting | bytes 12288

commit v4 on v3

--- a/solution.py
+++ b/solution.py
@@ -15,7 +15,6 @@
 LANES = 128
 GROUPS = NB // 2
 NEAR = 26
-CAP = 32
 AXES = ("gx", "gy", "gz")
 MESH = pl.DeviceIdType.MESH
 
@@ -269,6 +268,7 @@
 CHUNK = 16
 SHAPED = 1
 SUMMED = 4
+PUSHED = 4
 
 
 def code_of(n):
@@ -287,10 +287,15 @@
     return tuple(found)
 
 
+CAPS = [32 if sum(abs(step) for step in steps_of(code_of(n))) == 1 else 16 for n in range(NEAR)]
+BASE = [sum(CAPS[:n]) for n in range(NEAR)]
+TAKEN = sum(CAPS)
+FACES = [n for n in range(NEAR) if CAPS[n] == 32]
+
 FAR_FIRST = sorted(range(NEAR), key=lambda n: -sum(abs(step) for step in steps_of(code_of(n))))
 
 
-def started(neighbours, source_of, landing, first, send, receive):
+def started(neighbours, source_of, target_of, whole, send, receive):
     def copy_of(source, target, n):
         return pltpu.make_async_remote_copy(
             src_ref=source,
@@ -302,8 +307,7 @@
         )
 
     for n in FAR_FIRST:
-        copy_of(source_of(n), landing.at[first + NEAR - 1 - n], n).start()
-    whole = landing.at[pl.ds(first, NEAR)]
+        copy_of(source_of(n), target_of(NEAR - 1 - n), n).start()
     return [copy_of(whole, whole, 0)]
 
 
@@ -413,7 +417,7 @@
     over_pairs(pairs.shape[1], SHAPED, one_pair)
 
 
-def sum_pairs(with_force, pairs, chain, rows, radial, edges, weighted, running, pull, pushed, parted):
+def sum_pairs(pairs, chain, rows, radial, edges, weighted, running):
     def one_pair(pair, slot):
         before = chain[0, pair]
         near = rows[row_of(pairs[1, pair])]
@@ -426,18 +430,25 @@
             lines = slice(low * TILE, high * TILE)
             message = multiply(edges[pair, lines, :], weighted[slot, order])
             running[pair + 1, lines, :] = message + running[before, lines, :]
-        if with_force:
-            inner = across(rows[pairs[0, pair]], jnp.concatenate([near, near], axis=0))
-            line = iota((8, LANES), 0)
-            sums = jnp.zeros((8, LANES), jnp.float32)
-            for axis in range(3):
-                push = pull[pair, axis] * inner
-                pushed[pair + 1, axis] = push + pushed[before, axis]
-                summed = jnp.sum(push, axis=0, keepdims=True)
-                sums = jnp.where(line == axis, summed, sums)
-            parted[pair] = sums
 
     over_pairs(pairs.shape[1], SUMMED, one_pair)
+
+
+def push_pairs(pairs, chain, rows, pull, pushed, parted):
+    def one_pair(pair, slot):
+        before = chain[0, pair]
+        near = rows[row_of(pairs[1, pair])]
+        inner = across(rows[pairs[0, pair]], jnp.concatenate([near, near], axis=0))
+        line = iota((8, LANES), 0)
+        sums = jnp.zeros((8, LANES), jnp.float32)
+        for axis in range(3):
+            push = pull[pair, axis] * inner
+            pushed[pair + 1, axis] = push + pushed[before, axis]
+            summed = jnp.sum(push, axis=0, keepdims=True)
+            sums = jnp.where(line == axis, summed, sums)
+        parted[pair + 1] = sums + parted[chain[2, pair]]
+
+    over_pairs(pairs.shape[1], PUSHED, one_pair)
 
 
 def renewed(totals, hidden, mix, out_weight):
@@ -523,7 +534,6 @@
     channels = features_far.shape[1]
     slots = sources.shape[1]
     tiles = slots // TILE
-    taken = NEAR * CAP
     own_base = gathered.shape[0] - slots
     neighbours = [beside(n) for n in range(NEAR)]
     barrier = pltpu.get_barrier_semaphore()
@@ -543,8 +553,11 @@
     level32 = iota((32, slots), 0)
     tally = jnp.sum(jnp.where(code_row == level32, 1.0, 0.0), axis=1, keepdims=True)
     tally = jnp.where(iota((32, 1), 0) == 13, 0.0, tally)
+    room = jnp.full((32, 1), 16.0)
+    for n in FACES:
+        room = jnp.where(iota((32, 1), 0) == code_of(n), 32.0, room)
     flag = jnp.broadcast_to(
-        jnp.max(jnp.where(tally > CAP, 1.0, 0.0), axis=0, keepdims=True), (1, LANES)
+        jnp.max(jnp.where(tally > room, 1.0, 0.0), axis=0, keepdims=True), (1, LANES)
     )
     block[0:1, :] = row_all
     block[1:2, :] = jnp.zeros((1, slots), jnp.int32)
@@ -552,7 +565,7 @@
         block[1:2, 32 * layer : 32 * layer + 27] = wanted[layer : layer + 1, :]
     block[1:2, LANES : 2 * LANES] = flag.astype(jnp.int32)
     pl.semaphore_wait(barrier, NEAR)
-    copies = started(neighbours, lambda n: block, lists, 0, send_list, take_list)
+    copies = started(neighbours, lambda n: block, lambda n: lists.at[n], lists, send_list, take_list)
 
     newest = [jnp.int32(0)] * tiles
     for pair in range(pairs.shape[1]):
@@ -564,8 +577,19 @@
         chain[0, pair] = last
     for t in range(tiles):
         chain[1, t] = newest[t]
+    newest = [jnp.int32(0)] * (tiles + 27)
+    for pair in range(pairs.shape[1]):
+        source = pairs[1, pair]
+        last = jnp.int32(0)
+        for b in range(tiles + 27):
+            last = jnp.where(source == b, newest[b], last)
+            newest[b] = jnp.where(source == b, pair + 1, newest[b])
+        chain[2, pair] = last
+    for b in range(tiles + 27):
+        chain[3, b] = newest[b]
     running[0] = jnp.zeros(running.shape[1:], jnp.float32)
     pushed[0] = jnp.zeros(pushed.shape[1:], jnp.float32)
+    parted[0] = jnp.zeros(parted.shape[1:], jnp.float32)
     level = iota((LANES, LANES), 0)
     lane = iota((LANES, LANES), 1)
     for first in range(slots // LANES):
@@ -582,7 +606,10 @@
             total = total + jnp.where(same, 1.0, 0.0)
         rank = jnp.sum(total, axis=1, keepdims=True).astype(jnp.int32)
         neighbour = code - jnp.where(code >= 13, 1, 0)
-        index = jnp.where(code == 13, own_base + slot, neighbour * CAP + rank)
+        base = 16 * neighbour
+        for n in FACES:
+            base = base + jnp.where(neighbour > n, 16, 0)
+        index = jnp.where(code == 13, own_base + slot, base + rank)
         for part in range(gathered.shape[0] // LANES):
             hit = index == lane + part * LANES
             select[first * LANES : (first + 1) * LANES, part * LANES : (part + 1) * LANES] = (
@@ -592,7 +619,8 @@
     parts = three_parts(start)
     placed[:, 0:own_base] = jnp.zeros((8, own_base), jnp.float32)
     placed[:, own_base:] = start
-    gathered[taken:own_base, :] = jnp.zeros((own_base - taken, channels), jnp.bfloat16)
+    if own_base > TAKEN:
+        gathered[TAKEN:own_base, :] = jnp.zeros((own_base - TAKEN, channels), jnp.bfloat16)
     earlier = (iota((slots, slots), 0) < iota((slots, slots), 1)).astype(jnp.float32).astype(jnp.bfloat16)
     table[...] = jnp.zeros_like(table)
     spots_sent[...] = jnp.zeros_like(spots_sent)
@@ -613,27 +641,29 @@
     chosen = jnp.where(mine, 1.0, 0.0)
     rank = jnp.dot(chosen.astype(jnp.bfloat16), earlier, preferred_element_type=jnp.float32)
     rank = jnp.where(mine, rank, -1.0)
-    order = iota((CAP, slots), 0).astype(jnp.float32)
-    across_lane = iota((CAP, slots), 1).astype(jnp.float32)
+    order = iota((max(CAPS), slots), 0).astype(jnp.float32)
+    across_lane = iota((max(CAPS), slots), 1).astype(jnp.float32)
     own_features = gathered[own_base:, :]
     for n in range(NEAR):
-        hit = rank[n : n + 1, :] == order
+        hit = rank[n : n + 1, :] == order[0 : CAPS[n], :]
         place = jnp.sum(jnp.where(hit, slot[n : n + 1, :], 0.0), axis=1, keepdims=True)
-        picks[n * CAP : (n + 1) * CAP, :] = jnp.where(place == across_lane, 1.0, 0.0).astype(jnp.bfloat16)
+        picks[BASE[n] : BASE[n] + CAPS[n], :] = jnp.where(
+            place == across_lane[0 : CAPS[n], :], 1.0, 0.0
+        ).astype(jnp.bfloat16)
     sent = jnp.dot(picks[...], own_features, preferred_element_type=jnp.float32).astype(jnp.bfloat16)
-    rows_sent[...] = sent.reshape(rows_sent.shape)
+    rows_sent[...] = sent
     sent = joined(across(parts, picks[...]))
     for n in range(NEAR):
-        spots_sent[n, :, 0:CAP] = sent[:, n * CAP : (n + 1) * CAP]
+        spots_sent[n, :, 0 : CAPS[n]] = sent[:, BASE[n] : BASE[n] + CAPS[n]]
         spots_sent[n, 7:8, :] = flag
-    copies = started(neighbours, lambda n: rows_sent.at[n], rows_came, 0, send_moved, take_moved)
-    copies += started(neighbours, lambda n: spots_sent.at[n], spots_came, 0, send_spots, take_spots)
+    copies = started(neighbours, lambda n: rows_sent.at[pl.ds(BASE[n], CAPS[n])], lambda n: rows_came.at[pl.ds(BASE[n], CAPS[n])], rows_came, send_moved, take_moved)
+    copies += started(neighbours, lambda n: spots_sent.at[n], lambda n: spots_came.at[n], spots_came, send_spots, take_spots)
     fetch.wait()
     finish(copies)
 
-    gathered[0:taken, :] = rows_came[...].reshape(taken, channels)
+    gathered[0:TAKEN, :] = rows_came[...]
     for n in range(NEAR):
-        placed[:, n * CAP : (n + 1) * CAP] = spots_came[n, :, 0:CAP]
+        placed[:, BASE[n] : BASE[n] + CAPS[n]] = spots_came[n, :, 0 : CAPS[n]]
         flag = jnp.maximum(flag, spots_came[n, 7:8, :])
     moved = jnp.dot(select[...], gathered[...], preferred_element_type=jnp.float32).astype(jnp.bfloat16)
     hidden[...] = moved.reshape(hidden.shape)
@@ -659,8 +689,8 @@
         near = own_spots[wants[n, reader]]
         later = pltpu.roll(own_spots[wants[n, 32 + reader]], 3, 0)
         asked_spots[n] = jnp.where(line8 < 3, near, jnp.where(line8 < 6, later, flag))
-    placing = started(neighbours, lambda n: asked_spots.at[n], near_spots, 0, send_near, take_near)
-    copies = started(neighbours, lambda n: asked_first.at[n], rows_first, tiles, send_first, take_first)
+    placing = started(neighbours, lambda n: asked_spots.at[n], lambda n: near_spots.at[n], near_spots, send_near, take_near)
+    copies = started(neighbours, lambda n: asked_first.at[n], lambda n: rows_first.at[tiles + n], rows_first.at[pl.ds(tiles, NEAR)], send_first, take_first)
     rows_first[0:tiles] = own_rows[...]
     for t in range(tiles):
         own = own_spots[t]
@@ -680,7 +710,7 @@
 
     shape_pairs(False, pairs, force_weight, spots.at[0], wide, edges, pull)
     finish(copies)
-    sum_pairs(False, pairs, chain, rows_first, radial.at[0], edges, weighted, running, pull, pushed, parted)
+    sum_pairs(pairs, chain, rows_first, radial.at[0], edges, weighted, running)
     for t in range(tiles):
         new = renewed(running[chain[1, t]], hidden[t], mix[:, 0], out_weight[0])
         hidden[t] = new
@@ -689,30 +719,21 @@
         own_rows[t] = later
     for n in range(NEAR):
         asked_last[n] = own_rows[wants[n, 32 + 26 - code_of(n)]]
-    copies = started(neighbours, lambda n: asked_last.at[n], rows_last, tiles, send_last, take_last)
+    copies = started(neighbours, lambda n: asked_last.at[n], lambda n: rows_last.at[tiles + n], rows_last.at[pl.ds(tiles, NEAR)], send_last, take_last)
     shape_pairs(True, pairs, force_weight, spots.at[1], wide, edges, pull)
     finish(copies)
 
-    sum_pairs(True, pairs, chain, rows_last, radial.at[1], edges, weighted, running, pull, pushed, parted)
+    push_pairs(pairs, chain, rows_last, pull, pushed, parted)
     factor = 0.5 / math.sqrt(channels)
 
-    def add_part(pair, carried):
-        source = pairs[1, pair]
-        part = parted[pair]
-        return tuple(
-            held + jnp.where(source == b, part, jnp.zeros_like(part)) for b, held in enumerate(carried)
-        )
-
-    sums = lax.fori_loop(
-        0,
-        pairs.shape[1],
-        add_part,
-        tuple(jnp.zeros((8, LANES), jnp.float32) for _ in range(tiles + 27)),
-    )
-    sums = [(held + pltpu.roll(held, TILE, 1)) * factor for held in sums]
+    def returned(b):
+        held = parted[chain[3, b]]
+        return (held + pltpu.roll(held, TILE, 1)) * factor
+
     for n in range(NEAR):
-        force_sent[n] = jnp.where(line8 < 7, -sums[tiles + code_of(n)], flag)
-    copies = started(neighbours, lambda n: force_sent.at[n], force_came, 0, send_force, take_force)
+        force_sent[n] = jnp.where(line8 < 7, -returned(tiles + code_of(n)), flag)
+    copies = started(neighbours, lambda n: force_sent.at[n], lambda n: force_came.at[n], force_came, send_force, take_force)
+    sum_pairs(pairs, chain, rows_last, radial.at[1], edges, weighted, running)
     lane64 = iota((TILE, LANES), 1)
     for t in range(tiles):
         updated[t * TILE : (t + 1) * TILE, :] = renewed(running[chain[1, t]], hidden[t], mix[:, 1], out_weight[1])
@@ -721,7 +742,7 @@
         for axis in range(3):
             columns = jnp.where(lane64 == axis, jnp.sum(push[axis], axis=1, keepdims=True), columns)
         turned = jnp.transpose(jnp.concatenate([columns, columns], axis=0))[0:8, :]
-        own_force[t] = turned * factor - sums[t]
+        own_force[t] = turned * factor - returned(t)
     finish(copies)
     totals = [own_force[t] for t in range(tiles)]
     for n in range(NEAR):
@@ -754,7 +775,7 @@
     tiles = slots // TILE
     edge = float((slots / DENSITY) ** (1.0 / 3.0))
     count = pairs.shape[4]
-    held = -(-NEAR * CAP // LANES) * LANES + slots
+    held = -(-TAKEN // LANES) * LANES + slots
     shape = jax.ShapeDtypeStruct
     far, bits = jnp.float32, jnp.bfloat16
 
@@ -775,10 +796,10 @@
             pltpu.VMEM((2, slots), jnp.int32),
             pltpu.VMEM((NEAR, 2, slots), jnp.int32),
             pltpu.VMEM((32, slots), jnp.int32),
-            pltpu.VMEM((NEAR * CAP, slots), bits),
-            pltpu.VMEM((NEAR, CAP, channels), bits),
+            pltpu.VMEM((TAKEN, slots), bits),
+            pltpu.VMEM((TAKEN, channels), bits),
             pltpu.VMEM((NEAR, 8, LANES), far),
-            pltpu.VMEM((NEAR, CAP, channels), bits),
+            pltpu.VMEM((TAKEN, channels), bits),
             pltpu.VMEM((NEAR, 8, LANES), far),
             pltpu.VMEM((held, channels), bits),
             pltpu.VMEM((8, held), far),
@@ -799,14 +820,14 @@
             pltpu.VMEM((SUMMED, 3, NB * TILE, channels), bits),
             pltpu.VMEM((count + 1, 9 * TILE, channels), far),
             pltpu.VMEM((count + 1, 3, TILE, LANES), far),
-            pltpu.VMEM((count, 8, LANES), far),
+            pltpu.VMEM((count + 1, 8, LANES), far),
             pltpu.VMEM((NEAR, 8, LANES), far),
             pltpu.VMEM((NEAR, 8, LANES), far),
             pltpu.VMEM((tiles, 8, LANES), far),
             pltpu.VMEM((LAYERS, channels, channels), bits),
             pltpu.VMEM((LAYERS, channels, channels), bits),
             pltpu.SMEM((NEAR, LANES), jnp.int32),
-            pltpu.SMEM((2, LANES), jnp.int32),
+            pltpu.SMEM((4, LANES), jnp.int32),
             pltpu.SemaphoreType.DMA((4,)),
         ]
         + [pltpu.SemaphoreType.DMA] * 14,
@@ -828,6 +849,20 @@
     )
     updated = updated.reshape(features.shape)
     forces = forces.reshape(coords.shape)
+    def settled():
+        def settle(rows_in, forces_in, rows_out, forces_out):
+            rows_out[...] = rows_in[...]
+            forces_out[...] = forces_in[...]
+
+        rows, pushes = pl.pallas_call(
+            settle,
+            name="settle",
+            out_shape=[shape((slots, channels), bits), shape((1, 3 * slots), far)],
+            in_specs=[VMEM] * 2,
+            out_specs=[VMEM] * 2,
+        )(updated.reshape(slots, channels), forces.reshape(1, 3 * slots))
+        return (rows.reshape(features.shape), pushes.reshape(coords.shape))
+
     return lax.cond(
         flag[0, 0] > 0,
         lambda: whole_path(
@@ -843,7 +878,7 @@
             out_weight,
             force_weight,
         ),
-        lambda: (updated, forces),
+        settled,
     )
 
 

time: 73.7 us -> 67.6 us (0.917)
  Pallas kernels: 68.4 us -> 64.8 us
  local copies, waits for them, and re-layouts: 2.85 us -> 0.59 us
    pallas_call x1, Pallas kernels: 68.4 us -> 64.1 us  [body(): pl.pallas_call(kernel, name='whole_step', out_shape=[shape((slots, channe...]
    unnamed x2, local copies, waits for them, and re-layouts: 2.85 us -> 0.59 us
where the time goes in v4:
time: 67.6 us; the launch traced here: 67.4 us
  Pallas kernels  64.8 us (96%)
  between operations  1.97 us (3%)
    pallas_call x1, Pallas kernels, body(): pl.pallas_call(kernel, name='whole_step', out_shape=[shape((slots, channe...  64.1 us

profile of v4, /device:TPU:1, one launch (start us, length us, event | category | flops | bytes accessed | tf_op | source)
XLA Modules:
  0.0 67.4 jit_solution(15838869735923199867)
XLA Ops:
  1.3 64.1 %whole_step.1 = (bf16[512,128]{1,0:T(8,128)(2,1)S(1)}, f32[1,1536]{1,0:T(1,128)S(1)}, s32[1,128]{1,0:T(1,128)}) custom-call(s32[1]{0:T(128)} %bitcast.316.refs_0_, s32[2,32]{1,0:T(2,128)} %bitcast.353, f32[8]{0:T(128)} %refs_2_.1, s32[1,512]{1,0:T(1,128)} %bitcast.356, s32[2,27]{1,0:T(2,128)} %bitcast.358, f32[1,1536]{1,0:T(1,128)} %bitcast.362, ...), custom_call_target="tpu_custom_call" | custom-call | tf_op jit(solution)/shard_map/whole_step/pallas_call | solution.py:785
  66.1 0.7 %conditional.1 = (bf16[512,128]{1,0:T(8,128)(2,1)}, f32[1,1,1,3,512]{4,2,3,1,0:T(1,128)S(1)}) conditional(s32[]{:T(128)} %bitcast.109, (bf16[512,128]{1,0:T(8,128)(2,1)S(1)}, f32[1,1536]{1,0:T(1,128)S(1)}) %tuple.61, (s32[1,1,1,512]{3,2,1,0:T(1,128)}, bf16[1,1,1,512,128]{4,3,2,1,0:T(8,128)(2,1)}, f32[2,3,128]{2,0,1:T(2,128)}, ...), branch_computations={%region_0.0_spmd, %region_1.21_spmd} | conditional | flops 401764960 | bytes 138199456 | solution.py:866
  66.1 0.7 settle.1
  66.8 0.0 copy-start.42
  66.8 0.6 copy-done.42
Async XLA Ops:
  66.8 0.6 copy-start.42
